TPU v7x, 256 devices: a whole 4x4x8 slice. The times are simulated.
256 devices in a mesh: member: 64 (over z, y, x_lo), dp: 4 (over x_hi, core).
Axes of the slice: x: 4 (x_hi: 2, x_lo: 2; x = x_hi * 2 + x_lo), y: 4, z: 8, core: 2. Of those that a mesh axis runs over, the one named last changes fastest.
Arguments:
- tokens: bfloat16 [64, 16, 196, 768], P('member', 'dp'), may hold values from -6 to 6
- labels: int32 [64, 16], P('member', 'dp'), may hold values from 0 to 499
- source: int32 [64], replicated, may hold values from 0 to 63, as said below
- learn_rate: float32 [64], P('member'), may hold values from 0.02 to 0.2
- weight_decay: float32 [64], P('member'), may hold values from 0.1 to 1
- classifier: bfloat16 [768, 500], replicated, may hold values from -8 to 8
- up_param: float32 [64, 768, 1536], P('member', 'dp'), may hold values from -6 to 6
- up_first: bfloat16 [64, 768, 1536], P('member', 'dp'), may hold values from -0.005859375 to 0.005859375
- up_second: float32 [64, 768, 1536], P('member', 'dp'), may hold values from 1e-07 to 1e-05
- down_param: float32 [64, 1536, 768], P('member', 'dp'), may hold values from -6 to 6
- down_first: bfloat16 [64, 1536, 768], P('member', 'dp'), may hold values from -0.005859375 to 0.005859375
- down_second: float32 [64, 1536, 768], P('member', 'dp'), may hold values from 1e-07 to 1e-05
Outputs:
- up_weight: float32 [64, 768, 1536], P('member', 'dp')
- up_moment: bfloat16 [64, 768, 1536], P('member', 'dp')
- up_variance: float32 [64, 768, 1536], P('member', 'dp')
- down_weight: float32 [64, 1536, 768], P('member', 'dp')
- down_moment: bfloat16 [64, 1536, 768], P('member', 'dp')
- down_variance: float32 [64, 1536, 768], P('member', 'dp')
Inputs may be any that keep to these rules, and one draw needn't show every extreme that they name: source[i] = i except for the 16 members of the lowest quartile of a ranking; each of those names a member of the highest quartile, which keeps its own index; a winner may be named by several losers.
All inputs are finite; a program needn't handle non-finite values.
Results may differ from a plain program's by a relative error of at most 0.009.
Values may be sent and summed in bfloat16 or wider, within the bound.
A program may use at most 128 MiB of HBM per device.

v0:
```python
import functools

import jax
import jax.numpy as jnp
from jax import lax
from jax.experimental import pallas as pl
from jax.experimental.pallas import tpu as pltpu
from jax.sharding import PartitionSpec as P

MESH_ID = pl.DeviceIdType.MESH

STEP = 1000


def local_gradients(tokens, labels, up_weight, down_weight, classifier, batch_total):
    images, patches, features = tokens.shape
    hidden_units = up_weight.shape[1]
    token_rows = tokens.reshape(images * patches, features).astype(jnp.float32)
    center = token_rows - jnp.mean(token_rows, axis=1, keepdims=True)
    normed = (center * lax.rsqrt(jnp.mean(center * center, axis=1, keepdims=True) + 1e-06)).astype(
        jnp.bfloat16
    )
    preact = jnp.dot(normed, up_weight, preferred_element_type=jnp.float32) * features ** (-0.5)
    activated = (0.5 * preact * (1.0 + lax.erf(preact * 0.7071067811865476))).astype(jnp.bfloat16)
    residual = token_rows + jnp.dot(
        activated, down_weight, preferred_element_type=jnp.float32
    ) * hidden_units ** (-0.5)
    out_center = residual - jnp.mean(residual, axis=1, keepdims=True)
    inverse = lax.rsqrt(jnp.mean(out_center * out_center, axis=1, keepdims=True) + 1e-06)
    out_normed = out_center * inverse
    pooled = jnp.mean(out_normed.reshape(images, patches, features), axis=1).astype(jnp.bfloat16)
    logits = jnp.dot(pooled, classifier, preferred_element_type=jnp.float32)
    powered = jnp.exp(logits)
    softmax_out = powered / jnp.sum(powered, axis=1, keepdims=True)
    onehot = (labels[:, None] == jnp.arange(classifier.shape[1], dtype=jnp.int32)[None, :]).astype(
        jnp.float32
    )
    logit_delta = ((softmax_out - onehot) / batch_total).astype(jnp.bfloat16)
    pool_delta = (
        lax.dot_general(
            logit_delta, classifier, (((1,), (1,)), ((), ())), preferred_element_type=jnp.float32
        )
        / patches
    )
    token_delta = jnp.broadcast_to(pool_delta[:, None, :], (images, patches, features)).reshape(
        images * patches, features
    )
    residual_delta = inverse * (
        token_delta
        - jnp.mean(token_delta, axis=1, keepdims=True)
        - out_normed * jnp.mean(token_delta * out_normed, axis=1, keepdims=True)
    )
    residual_delta = residual_delta.astype(jnp.bfloat16)
    down_scale = hidden_units ** (-0.5)
    down_gradient = (
        lax.dot_general(
            activated, residual_delta, (((0,), (0,)), ((), ())), preferred_element_type=jnp.float32
        )
        * down_scale
    )
    hidden_delta = (
        lax.dot_general(
            residual_delta,
            down_weight,
            (((1,), (1,)), ((), ())),
            preferred_element_type=jnp.float32,
        )
        * down_scale
    )
    derivative = (
        0.5 * (1.0 + lax.erf(preact * 0.7071067811865476))
        + preact * jnp.exp(-0.5 * preact * preact) * 0.3989422804014327
    )
    preact_delta = (hidden_delta * derivative).astype(jnp.bfloat16)
    up_gradient = lax.dot_general(
        normed, preact_delta, (((0,), (0,)), ((), ())), preferred_element_type=jnp.float32
    ) * features ** (-0.5)
    return (up_gradient, down_gradient)


def adamw_step(param, first, second, gradient, rate_value, decay_value):
    moment = 0.9 * first.astype(jnp.float32) + 0.1 * gradient
    variance = 0.999 * second + 0.001 * gradient * gradient
    update = (
        moment / (1.0 - 0.9**STEP) / (jnp.sqrt(variance / (1.0 - 0.999**STEP)) + 1e-08)
        + decay_value * param
    )
    return (param - rate_value * update, moment.astype(jnp.bfloat16), variance)


def enter(n, me):
    barrier = pltpu.get_barrier_semaphore()

    def greet(k, carry):
        pl.semaphore_signal(
            barrier, inc=1, device_id={"member": lax.rem(me + k, n)}, device_id_type=MESH_ID
        )
        return carry

    lax.fori_loop(1, n, greet, 0)
    pl.semaphore_wait(barrier, n - 1)


def transpose(n, me, src, dst, send_sem, recv_sem):
    def copy(k):
        target = lax.rem(me + k, n)
        return pltpu.make_async_remote_copy(
            src_ref=src.at[target],
            dst_ref=dst.at[me],
            send_sem=send_sem.at[k],
            recv_sem=recv_sem.at[k],
            device_id={"member": target},
            device_id_type=MESH_ID,
        )

    def start(k, carry):
        copy(k).start()
        return carry

    def finish(k, carry):
        copy(k).wait()
        return carry

    lax.fori_loop(1, n, start, 0)
    dst[me] = src[me]
    lax.fori_loop(1, n, finish, 0)


def pick_rows(n, source_ref, held, picked):
    def pick(i, carry):
        picked[i] = held[source_ref[i]]
        return carry

    lax.fori_loop(0, n, pick, 0)


def exploit_kernel(n, source_ref, send_ref, out_ref, held, picked, send1, recv1, send2, recv2):
    me = lax.axis_index("member")
    enter(n, me)
    transpose(n, me, send_ref, held, send1, recv1)
    pick_rows(n, source_ref, held, picked)
    transpose(n, me, picked, out_ref, send2, recv2)


def gather_kernel(n, source_ref, send_ref, out_ref, held, send1, recv1):
    me = lax.axis_index("member")
    enter(n, me)
    transpose(n, me, send_ref, held, send1, recv1)
    pick_rows(n, source_ref, held, out_ref)


def scatter_kernel(n, send_ref, out_ref, send1, recv1):
    me = lax.axis_index("member")
    enter(n, me)
    transpose(n, me, send_ref, out_ref, send1, recv1)


def member_call(body, packed, operands, scratch, kernel_id):
    n, rows, lanes = packed.shape
    moved = packed.size * packed.dtype.itemsize
    smem = [pl.BlockSpec(memory_space=pltpu.SMEM)] * (len(operands) - 1)
    return pl.pallas_call(
        functools.partial(body, n),
        out_shape=jax.ShapeDtypeStruct(packed.shape, packed.dtype),
        in_specs=smem + [pl.BlockSpec(memory_space=pltpu.VMEM)],
        out_specs=pl.BlockSpec(memory_space=pltpu.VMEM),
        scratch_shapes=scratch,
        compiler_params=pltpu.CompilerParams(
            collective_id=kernel_id, has_side_effects=True, vmem_limit_bytes=48 * 1024 * 1024
        ),
        cost_estimate=pl.CostEstimate(flops=0, transcendentals=0, bytes_accessed=moved * 20),
    )(*operands)


def exploit_transfer(packed, source, kernel_id):
    n, rows, lanes = packed.shape
    block = pltpu.VMEM((n, rows, lanes), packed.dtype)
    sems = [pltpu.SemaphoreType.DMA((n,))] * 4
    return member_call(exploit_kernel, packed, (source, packed), [block, block] + sems, kernel_id)


def exploit_gather(packed, source, kernel_id):
    n, rows, lanes = packed.shape
    block = pltpu.VMEM((n, rows, lanes), packed.dtype)
    sems = [pltpu.SemaphoreType.DMA((n,))] * 2
    return member_call(gather_kernel, packed, (source, packed), [block] + sems, kernel_id)


def exploit_scatter(packed, kernel_id):
    n = packed.shape[0]
    sems = [pltpu.SemaphoreType.DMA((n,))] * 2
    return member_call(scatter_kernel, packed, (packed,), sems, kernel_id)


def lane_major(part, lanes):
    rows, cols = part.shape
    return part.reshape(rows, cols // lanes, lanes).transpose(1, 0, 2).reshape(-1, lanes)


def from_lane_major(flat, shape, lanes):
    rows, cols = shape
    return flat.reshape(cols // lanes, rows, lanes).transpose(1, 0, 2).reshape(rows, cols)


def exploit_rows(parts, source, members, kernel_id):
    lanes = 128
    rows = [part.size // (members * lanes) for part in parts]
    pad = -sum(rows) % 16
    pieces = [part.astype(jnp.bfloat16).reshape(members, -1, lanes) for part in parts]
    if pad:
        pieces.append(jnp.zeros((members, pad, lanes), jnp.bfloat16))
    back = exploit_transfer(jnp.concatenate(pieces, axis=1), source, kernel_id)
    out = []
    start = 0
    for part, count in zip(parts, rows):
        out.append(back[:, start:start + count].reshape(part.shape))
        start += count
    return out


def pack_tiles(parts, members):
    lanes = 128
    flat = jnp.concatenate([lane_major(part.astype(jnp.bfloat16), lanes) for part in parts])
    return flat.reshape(members, -1, flat.shape[-1])


def unpack_tiles(back, parts):
    lanes = back.shape[-1]
    back = back.reshape(-1, lanes)
    out = []
    start = 0
    for part in parts:
        count = part.size // lanes
        out.append(from_lane_major(back[start:start + count], part.shape, lanes))
        start += count
    return out


def per_device(
    tokens,
    labels,
    source,
    learn_rate,
    weight_decay,
    classifier,
    up_param,
    up_first,
    up_second,
    down_param,
    down_first,
    down_second,
):
    members = lax.axis_size("member")
    shards = lax.axis_size("dp")
    me = lax.axis_index("member")
    own = source[me] == me

    up_bf, down_bf = exploit_rows((up_param[0], down_param[0]), source, members, 0)
    up_full = lax.all_gather(up_bf, "dp", axis=0, tiled=True)
    down_full = lax.all_gather(down_bf, "dp", axis=0, tiled=True)
    moments = (up_first[0], down_first[0], up_second[0], down_second[0])
    picked = exploit_gather(pack_tiles(moments, members), source, 1)
    up_full, down_full, picked = lax.optimization_barrier((up_full, down_full, picked))

    batch_total = tokens.shape[1] * shards
    up_gradient, down_gradient = local_gradients(
        tokens[0], labels[0], up_full, down_full, classifier, batch_total
    )
    up_term = up_gradient.astype(jnp.bfloat16)
    down_term = down_gradient.astype(jnp.bfloat16)
    up_term, down_term, picked = lax.optimization_barrier((up_term, down_term, picked))
    up_share = lax.psum_scatter(up_term, "dp", scatter_dimension=0, tiled=True)
    down_share = lax.psum_scatter(down_term, "dp", scatter_dimension=0, tiled=True)
    up_mom, down_mom, up_var_bf, down_var_bf = unpack_tiles(exploit_scatter(picked, 2), moments)
    up_share = up_share.astype(jnp.float32)
    down_share = down_share.astype(jnp.float32)

    up_now = jnp.where(own, up_param[0], up_bf.astype(jnp.float32))
    down_now = jnp.where(own, down_param[0], down_bf.astype(jnp.float32))
    up_var = jnp.where(own, up_second[0], up_var_bf.astype(jnp.float32))
    down_var = jnp.where(own, down_second[0], down_var_bf.astype(jnp.float32))

    rate_value = learn_rate[0]
    decay_value = weight_decay[0]
    up_new = adamw_step(up_now, up_mom, up_var, up_share, rate_value, decay_value)
    down_new = adamw_step(down_now, down_mom, down_var, down_share, rate_value, decay_value)
    return tuple(value[None] for value in up_new + down_new)


def solution(mesh):
    placed = (
        P("member", "dp", None, None),
        P("member", "dp"),
        P(),
        P("member"),
        P("member"),
        P(),
        P("member", "dp", None),
        P("member", "dp", None),
        P("member", "dp", None),
        P("member", "dp", None),
        P("member", "dp", None),
        P("member", "dp", None),
    )
    return jax.shard_map(
        per_device,
        mesh=mesh,
        in_specs=placed,
        out_specs=(P("member", "dp", None),) * 6,
        check_vma=False,
    )
```

profile of v0, /device:TPU:1, one launch (start us, length us, event | category | flops | bytes accessed | tf_op | source)
XLA Modules:
  0.0 343.0 jit_solution(10080236754694199541)
XLA Ops:
  7.2 1.5 convert_element_type.121
  8.7 0.6 convert_element_type.122
  9.3 0.1 convert_element_type.119
  9.4 0.7 convert_element_type.120
  10.1 0.1 pad.6.clone
  10.2 0.5 maximum_maximum_fusion.send_ref
  10.7 72.5 %shard_map.163 = bf16[64,80,128]{2,1,0:T(8,128)(2,1)S(1)} custom-call(s32[64]{0:T(128)S(1)} %copy-done.2, bf16[64,80,128]{2,1,0:T(8,128)(2,1)S(1)} %maximum_maximum_fusion.send_ref), custom_call_target="tpu_custom_call" | custom-call | bytes 26214400 | tf_op jit(solution)/shard_map/pallas_call | solution.py:162
  83.2 1.1 fusion.23
  84.3 1.5 reshape.153
  85.8 0.0 all-gather.5.cloned.1.call-start
  85.9 2.5 reshape.154
  88.4 0.2 reduce-scatter.3.cloned.1.call-start
  88.7 1.1 copy.74
  89.7 1.4 copy.75
  91.1 0.1 convert_element_type.128
  91.2 0.4 convert_element_type.129
  91.6 1.0 copy.73
  92.6 1.4 copy.71
  94.0 0.4 copy.72
  94.3 1.5 reshape_squeeze.7
  95.8 0.2 copy.70
  96.0 11.3 %pad_maximum_fusion = bf16[9216,128]{1,0:T(8,128)(2,1)S(1)} fusion(bf16[2304,128]{1,0:T(8,128)(2,1)S(1)} %bitcast.107, bf16[2304,128]{1,0:T(8,128)(2,1)} %bitcast.109, bf16[2304,128]{1,0:T(8,128)(2,1)S(1)} %bitcast.108, bf16[2304,128]{1,0:T(8,128)(2,1)S(1)} %bitcast.110), kind=kLoop, calls=%fused_computation.11 | loop fusion | flops 9437184 | bytes 4718592 | tf_op jit(solution)/shard_map/concatenate | solution.py:223
  107.3 62.5 %shard_map.164.send_ref = bf16[64,144,128]{2,1,0:T(8,128)(2,1)S(1)} custom-call(s32[64]{0:T(128)S(1)} %copy-done.2, bf16[64,144,128]{2,1,0:T(8,128)(2,1)S(1)} %bitcast.98), custom_call_target="tpu_custom_call" | custom-call | bytes 47185920 | tf_op jit(solution)/shard_map/pallas_call | solution.py:162
  169.9 1.6 copy.66
  171.5 2.9 reshape.162
  174.4 1.8 convert_reduce_fusion
  176.3 0.1 copy.84
  176.4 2.4 multiply_reduce_fusion.2
  178.8 0.1 copy.85
  178.9 0.1 rsqrt.20
  179.0 0.1 div.65
  179.1 6.2 %multiply_convert_fusion.1 = (bf16[784,1536]{1,0:T(8,128)(2,1)S(1)}, f32[784,1536]{1,0:T(8,128)}) fusion(bf16[768,1536]{1,0:T(8,128)(2,1)} %all-gather.3.cloned.1.call-done, f32[784,768]{1,0:T(8,128)} %reshape.162, f32[784]{0:T(1024)S(1)} %rsqrt.20, f32[784]{0:T(1024)S(1)} %div.65), kind=kOutput, calls=%fused_computation.1 | convolution fusion | flops 1857515520 | bytes 11999360 | tf_op jit(solution)/shard_map/dot_general | solution.py:23
  185.3 2.2 fusion.24
  187.6 0.5 multiply_reduce_fusion.1
  188.0 1.0 copy-done.3
  189.0 1.7 subtract_multiply_fusion
  190.7 2.9 reshape.160
  193.6 1.8 reduce_sum.78
  195.4 0.4 fusion.25
  195.8 0.4 fusion.26
  196.2 1.6 broadcast_in_dim.17
  197.9 2.8 reshape.161
  200.7 2.9 multiply_reduce_fusion
  203.6 0.1 reduce_sum.81
  203.7 0.1 div.76
  203.8 2.9 multiply_convert_fusion.4
  206.7 1.1 copy-done.11
  207.8 4.0 %multiply_convert_fusion.2 = bf16[1536,768]{1,0:T(8,128)(2,1)} fusion(bf16[784,1536]{1,0:T(8,128)(2,1)S(1)} %copy-done.15, bf16[784,768]{1,0:T(8,128)(2,1)S(1)} %multiply_convert_fusion.4), kind=kOutput, calls=%fused_computation.3 | convolution fusion | flops 1852047360 | bytes 5971968 | tf_op jit(solution)/shard_map/dot_general | solution.py:56
  211.7 11.0 %multiply_convert_fusion.3 = bf16[768,1536]{1,0:T(8,128)(2,1)} fusion(f32[784,1536]{1,0:T(8,128)} %get-tuple-element.31, bf16[784,768]{1,0:T(8,128)(2,1)} %copy-done.11, bf16[1536,768]{1,0:T(8,128)(2,1)} %all-gather.5.cloned.1.call-done, f32[784,768]{1,0:T(8,128)} %reshape.162, f32[784]{0:T(1024)S(1)} %rsqrt.20, f32[784]{0:T(1024)S(1)} %div.65), kind=kOutput, calls=%fused_computation.4 | convolution fusion | flops 3717992448 | bytes 13154432 | tf_op jit(solution)/shard_map/dot_general | solution.py:75
  222.8 0.0 reduce-scatter.5.cloned.1.call-start
  222.8 0.5 reduce-scatter.5.cloned.1.call-update
  223.4 0.6 dynamic_slice.3
  225.9 63.6 %shard_map.165 = bf16[64,144,128]{2,1,0:T(8,128)(2,1)S(1)} custom-call(bf16[64,144,128]{2,1,0:T(8,128)(2,1)S(1)} %shard_map.164.send_ref), custom_call_target="tpu_custom_call" | custom-call | bytes 47185920 | tf_op jit(solution)/shard_map/pallas_call | solution.py:162
  289.6 0.1 fusion.22
  289.7 0.4 copy.77
  290.0 0.2 convert_multiply_fusion.2
  290.2 2.0 copy.76
  292.2 1.3 copy.80
  293.4 2.7 copy.81
  296.1 1.4 copy.78
  297.5 2.7 copy.79
  300.1 5.9 %fusion.20 = (f32[1,192,1536]{2,1,0:T(8,128)}, f32[1,192,1536]{2,1,0:T(8,128)}, bf16[1,192,1536]{2,1,0:T(8,128)(2,1)}) fusion(bf16[192,1536]{1,0:T(8,128)(2,1)} %reduce-scatter.3.cloned.1.call-done, f32[24,8,12,128]{3,2,1,0:T(8,128)S(1)} %bitcast.99, f32[1,192,1536]{2,1,0:T(8,128)} %param.20, pred[]{:T(512)S(6)} %eq.18, f32[]{:T(128)} %bitcast.96, ...), kind=kLoop, calls=%fused_computation.60 | loop fusion | flops 5308416 | bytes 8847369 | tf_op jit(solution)/shard_map/broadcast_in_dim | solution.py:287
  306.0 25.6 %reduce-scatter.5.cloned.1.call-done = bf16[384,768]{1,0:T(8,128)(2,1)} async-done(((bf16[1536,768]{1,0:T(8,128)(2,1)}), bf16[384,768]{1,0:T(8,128)(2,1)}) %reduce-scatter.5.cloned.1.call-update) | async-done | bytes 589840 | tf_op jit(solution)/shard_map/reduce_scatter | solution.py:273
  331.6 4.9 %fusion.8 = (f32[1,384,768]{2,1,0:T(8,128)}, f32[1,384,768]{2,1,0:T(8,128)}, bf16[1,384,768]{2,1,0:T(8,128)(2,1)}) fusion(bf16[384,768]{1,0:T(8,128)(2,1)} %reduce-scatter.5.cloned.1.call-done, f32[384,768]{1,0:T(8,128)} %copy.81, f32[1,384,768]{2,1,0:T(8,128)} %param.23, pred[]{:T(512)S(6)} %eq.18, f32[]{:T(128)} %bitcast.97, f32[384,768]{1,0:T(8,128)} %copy.79, ...), kind=kLoop, calls=%fused_computation.38 | loop fusion | flops 5308416 | bytes 8847369 | tf_op jit(solution)/shard_map/broadcast_in_dim | solution.py:287
  (44 shorter events, 0.2 us)
Async XLA Ops:
  7.2 188.2 %copy-start = (bf16[768,500]{0,1:T(8,128)(2,1)S(1)}, bf16[768,500]{0,1:T(8,128)(2,1)}, u32[]{:S(2)}) copy-start(bf16[768,500]{0,1:T(8,128)(2,1)} %param.17) | copy-start | bytes 2304004
  7.2 2.1 copy-start.7
  7.2 171.9 %all-gather.3.cloned.1.call-start = ((), (), s32[]{:S(2)}) async-start(), calls=%async_computation.2 | async-start | bytes 2949120 | tf_op jit(solution)/shard_map/all_gather | solution.py:259
  9.3 1.3 copy-start.2
  84.3 4.3 %copy-start.9 = (f32[1,384,768]{2,1,0:T(8,128)S(1)}, f32[1,384,768]{2,1,0:T(8,128)}, u32[]{:S(2)}) copy-start(f32[1,384,768]{2,1,0:T(8,128)} %param.23) | copy-start | bytes 3538948
  85.8 93.3 %all-gather.5.cloned.1.call-start = ((), (), s32[]{:S(2)}) async-start(), calls=%async_computation.3 | async-start | bytes 2949120 | tf_op jit(solution)/shard_map/all_gather | solution.py:260
  85.9 5.2 %copy-start.8 = (f32[1,192,1536]{2,1,0:T(8,128)S(1)}, f32[1,192,1536]{2,1,0:T(8,128)}, u32[]{:S(2)}) copy-start(f32[1,192,1536]{2,1,0:T(8,128)} %param.20) | copy-start | bytes 3538948
  88.4 211.7 %reduce-scatter.3.cloned.1.call-start = ((), (), s32[]{:S(2)}) async-start(), calls=%async_computation.4 | async-start | bytes 2949120 | tf_op jit(solution)/shard_map/reduce_scatter | solution.py:272
  107.3 62.6 %copy-start.4 = (bf16[1,4,196,768]{3,1,2,0:T(4,128)(2,1)S(1)}, bf16[1,4,196,768]{3,1,2,0:T(4,128)(2,1)}, u32[]{:S(2)}) copy-start(bf16[1,4,196,768]{3,1,2,0:T(4,128)(2,1)} %param.12) | copy-start | bytes 3612676
  179.1 6.2 %copy-start.10 = (f32[784,768]{1,0:T(8,128)S(1)}, f32[784,768]{1,0:T(8,128)}, u32[]{:S(2)}) copy-start(f32[784,768]{1,0:T(8,128)} %reshape.162) | copy-start | bytes 7225348
  179.1 6.2 %copy-start.12 = (bf16[1536,768]{1,0:T(8,128)(2,1)S(1)}, bf16[1536,768]{1,0:T(8,128)(2,1)}, u32[]{:S(2)}) copy-start(bf16[1536,768]{1,0:T(8,128)(2,1)} %all-gather.5.cloned.1.call-done) | copy-start | bytes 7077892
  185.3 2.2 copy-start.14
  187.5 1.5 copy-start.3
  193.6 2.3 copy-start.13
  203.8 4.0 %copy-start.15 = (bf16[784,1536]{1,0:T(8,128)(2,1)S(1)}, bf16[784,1536]{1,0:T(8,128)(2,1)}, u32[]{:S(2)}) copy-start(bf16[784,1536]{1,0:T(8,128)(2,1)} %copy-done.14) | copy-start | bytes 7225348
  206.7 1.1 copy-start.11
  222.8 108.8 %reduce-scatter.5.cloned.1.call-start = ((), (), s32[]{:S(2)}) async-start(), calls=%async_computation.5 | async-start | bytes 2949120 | tf_op jit(solution)/shard_map/reduce_scatter | solution.py:273
  296.1 4.1 %copy-start.5 = (bf16[192,1536]{1,0:T(8,128)(2,1)S(1)}, bf16[192,1536]{1,0:T(8,128)(2,1)}, u32[]{:S(2)}) copy-start(bf16[192,1536]{1,0:T(8,128)(2,1)} %reshape.153) | copy-start | bytes 1769476
  300.1 31.4 %copy-start.6 = (bf16[384,768]{1,0:T(8,128)(2,1)S(1)}, bf16[384,768]{1,0:T(8,128)(2,1)}, u32[]{:S(2)}) copy-start(bf16[384,768]{1,0:T(8,128)(2,1)} %reshape.154) | copy-start | bytes 1769476
  331.5 5.0 %copy-start.1 = (bf16[768,500]{0,1:T(8,128)(2,1)S(1)}, bf16[768,500]{0,1:T(8,128)(2,1)}, u32[]{:S(2)}) copy-start(bf16[768,500]{0,1:T(8,128)(2,1)} %param.17) | copy-start | bytes 2304004
Sparse Core Ops, SparseCore 0:
  86.0 33.8 all-gather.2
  121.7 53.1 all-gather.4
  222.9 54.7 reduce-scatter.2
  280.6 50.8 reduce-scatter.4
where the time goes:
time: 344 us; the launch traced here: 343 us
  Pallas kernels  199 us (58%)
  local copies, waits for them, and re-layouts  39.1 us (11%)
  other arithmetic  38.5 us (11%)
  waiting for transfers between devices  26.1 us (8%)
  matrix products  24.2 us (7%)
  between operations  16.1 us (5%)
    pallas_call x3, Pallas kernels, member_call(): pl.pallas_call(functools.partial(body, n), out_shape=jax.ShapeDtypeStruct...  199 us
    reduce_scatter x1, waiting for transfers between devices, per_device(): lax.psum_scatter(down_term, 'dp', scatter_dimension=0, tiled=True)  25.6 us
    concatenate x1, other arithmetic, pack_tiles(): jnp.concatenate([lane_major(part.astype(jnp.bfloat16), lanes) for part in...  11.3 us
    dot_general x1, matrix products, local_gradients(): lax.dot_general(normed, preact_delta, (((0,), (0,)), ((), ())), preferred...  11 us
    broadcast_in_dim x2, other arithmetic, per_device(): return tuple((value[None] for value in up_new + down_new))  10.8 us
  transfers between devices with their start and end apart: 4, of which 1 were waited for; matrix products, arithmetic and copies ran while one was open for 14% of the time, Pallas kernels for 37%

commit v1 on v0

--- a/solution.py
+++ b/solution.py
@@ -153,6 +153,143 @@
     me = lax.axis_index("member")
     enter(n, me)
     transpose(n, me, send_ref, out_ref, send1, recv1)
+
+
+def block_gradients(tokens, labels_ref, up_weight, down_weight, classifier, batch_total, patches):
+    tokens_n, features = tokens.shape
+    hidden_units = up_weight.shape[1]
+    classes = classifier.shape[1]
+    images = tokens_n // patches
+    token_rows = tokens.astype(jnp.float32)
+    center = token_rows - jnp.mean(token_rows, axis=1, keepdims=True)
+    normed = (center * lax.rsqrt(jnp.mean(center * center, axis=1, keepdims=True) + 1e-06)).astype(
+        jnp.bfloat16
+    )
+    preact = jnp.dot(normed, up_weight, preferred_element_type=jnp.float32) * features ** (-0.5)
+    activated = (0.5 * preact * (1.0 + lax.erf(preact * 0.7071067811865476))).astype(jnp.bfloat16)
+    residual = token_rows + jnp.dot(
+        activated, down_weight, preferred_element_type=jnp.float32
+    ) * hidden_units ** (-0.5)
+    out_center = residual - jnp.mean(residual, axis=1, keepdims=True)
+    inverse = lax.rsqrt(jnp.mean(out_center * out_center, axis=1, keepdims=True) + 1e-06)
+    out_normed = out_center * inverse
+    image_of_row = lax.broadcasted_iota(jnp.int32, (tokens_n, 1), 0) // patches
+    pooled = jnp.concatenate(
+        [
+            jnp.sum(jnp.where(image_of_row == i, out_normed, 0.0), axis=0, keepdims=True)
+            for i in range(images)
+        ],
+        axis=0,
+    ) / patches
+    pooled = pooled.astype(jnp.bfloat16)
+    logits = jnp.dot(pooled, classifier, preferred_element_type=jnp.float32)
+    powered = jnp.exp(logits)
+    softmax_out = powered / jnp.sum(powered, axis=1, keepdims=True)
+    row = lax.broadcasted_iota(jnp.int32, (images, classes), 0)
+    column = lax.broadcasted_iota(jnp.int32, (images, classes), 1)
+    label = jnp.zeros((images, classes), jnp.int32)
+    for i in range(images):
+        label = jnp.where(row == i, labels_ref[i], label)
+    onehot = (column == label).astype(jnp.float32)
+    logit_delta = ((softmax_out - onehot) / batch_total).astype(jnp.bfloat16)
+    pool_delta = (
+        lax.dot_general(
+            logit_delta, classifier, (((1,), (1,)), ((), ())), preferred_element_type=jnp.float32
+        )
+        / patches
+    )
+    token_delta = jnp.zeros((tokens_n, features), jnp.float32)
+    for i in range(images):
+        token_delta = jnp.where(image_of_row == i, pool_delta[i:i + 1, :], token_delta)
+    residual_delta = inverse * (
+        token_delta
+        - jnp.mean(token_delta, axis=1, keepdims=True)
+        - out_normed * jnp.mean(token_delta * out_normed, axis=1, keepdims=True)
+    )
+    residual_delta = residual_delta.astype(jnp.bfloat16)
+    down_scale = hidden_units ** (-0.5)
+    down_gradient = (
+        lax.dot_general(
+            activated, residual_delta, (((0,), (0,)), ((), ())), preferred_element_type=jnp.float32
+        )
+        * down_scale
+    )
+    hidden_delta = (
+        lax.dot_general(
+            residual_delta, down_weight, (((1,), (1,)), ((), ())), preferred_element_type=jnp.float32
+        )
+        * down_scale
+    )
+    derivative = (
+        0.5 * (1.0 + lax.erf(preact * 0.7071067811865476))
+        + preact * jnp.exp(-0.5 * preact * preact) * 0.3989422804014327
+    )
+    preact_delta = (hidden_delta * derivative).astype(jnp.bfloat16)
+    up_gradient = lax.dot_general(
+        normed, preact_delta, (((0,), (0,)), ((), ())), preferred_element_type=jnp.float32
+    ) * features ** (-0.5)
+    return up_gradient, down_gradient
+
+
+def scatter_compute_kernel(
+    n, batch_total, patches, labels_ref, send_ref, tokens_ref, up_ref, down_ref, classifier_ref,
+    out_ref, up_grad_ref, down_grad_ref, send_sem, recv_sem,
+):
+    me = lax.axis_index("member")
+    enter(n, me)
+
+    def copy(k):
+        target = lax.rem(me + k, n)
+        return pltpu.make_async_remote_copy(
+            src_ref=send_ref.at[target],
+            dst_ref=out_ref.at[me],
+            send_sem=send_sem.at[k],
+            recv_sem=recv_sem.at[k],
+            device_id={"member": target},
+            device_id_type=MESH_ID,
+        )
+
+    def start(k, carry):
+        copy(k).start()
+        return carry
+
+    def finish(k, carry):
+        copy(k).wait()
+        return carry
+
+    lax.fori_loop(1, n, start, 0)
+    out_ref[me] = send_ref[me]
+    up_gradient, down_gradient = block_gradients(
+        tokens_ref[...], labels_ref, up_ref[...], down_ref[...], classifier_ref[...],
+        batch_total, patches,
+    )
+    up_grad_ref[...] = up_gradient.astype(up_grad_ref.dtype)
+    down_grad_ref[...] = down_gradient.astype(down_grad_ref.dtype)
+    lax.fori_loop(1, n, finish, 0)
+
+
+def scatter_with_gradients(picked, tokens, labels, up_full, down_full, classifier, batch_total,
+                           kernel_id):
+    n = picked.shape[0]
+    images, patches, features = tokens.shape
+    vmem = pl.BlockSpec(memory_space=pltpu.VMEM)
+    moved = picked.size * picked.dtype.itemsize
+    flops = 12 * images * patches * features * up_full.shape[1]
+    return pl.pallas_call(
+        functools.partial(scatter_compute_kernel, n, batch_total, patches),
+        out_shape=(
+            jax.ShapeDtypeStruct(picked.shape, picked.dtype),
+            jax.ShapeDtypeStruct(up_full.shape, jnp.bfloat16),
+            jax.ShapeDtypeStruct(down_full.shape, jnp.bfloat16),
+        ),
+        in_specs=[pl.BlockSpec(memory_space=pltpu.SMEM)] + [vmem] * 5,
+        out_specs=(vmem, vmem, vmem),
+        scratch_shapes=[pltpu.SemaphoreType.DMA((n,)), pltpu.SemaphoreType.DMA((n,))],
+        compiler_params=pltpu.CompilerParams(
+            collective_id=kernel_id, has_side_effects=True, vmem_limit_bytes=63 * 1024 * 1024
+        ),
+        cost_estimate=pl.CostEstimate(flops=flops, transcendentals=0, bytes_accessed=moved * 20),
+    )(labels, picked, tokens.reshape(images * patches, features), up_full, down_full, classifier)
 
 
 def member_call(body, packed, operands, scratch, kernel_id):
@@ -263,15 +400,12 @@
     up_full, down_full, picked = lax.optimization_barrier((up_full, down_full, picked))
 
     batch_total = tokens.shape[1] * shards
-    up_gradient, down_gradient = local_gradients(
-        tokens[0], labels[0], up_full, down_full, classifier, batch_total
-    )
-    up_term = up_gradient.astype(jnp.bfloat16)
-    down_term = down_gradient.astype(jnp.bfloat16)
-    up_term, down_term, picked = lax.optimization_barrier((up_term, down_term, picked))
+    back, up_term, down_term = scatter_with_gradients(
+        picked, tokens[0], labels[0], up_full, down_full, classifier, batch_total, 2
+    )
     up_share = lax.psum_scatter(up_term, "dp", scatter_dimension=0, tiled=True)
     down_share = lax.psum_scatter(down_term, "dp", scatter_dimension=0, tiled=True)
-    up_mom, down_mom, up_var_bf, down_var_bf = unpack_tiles(exploit_scatter(picked, 2), moments)
+    up_mom, down_mom, up_var_bf, down_var_bf = unpack_tiles(back, moments)
     up_share = up_share.astype(jnp.float32)
     down_share = down_share.astype(jnp.float32)
 

time: 344 us -> 347 us (level)
  waiting for transfers between devices: 26.1 us -> 80.5 us
  matrix products: 24.2 us -> 0 us
  local copies, waits for them, and re-layouts: 39.1 us -> 22.8 us
  other arithmetic: 38.5 us -> 26.8 us
    pallas_call x0 -> x1, Pallas kernels: none -> 65.5 us  [scatter_with_gradients(): pl.pallas_call(functools.partial(scatter_compute_kernel, n, batch_total,...]
    pallas_call x3 -> x2, Pallas kernels: 199 us -> 135 us  [member_call(): pl.pallas_call(functools.partial(body, n), out_shape=jax.ShapeDtypeStruct...]
    reduce_scatter x1, waiting for transfers between devices: 0.01 us -> 42.4 us  [per_device(): up_share = lax.psum_scatter(up_term, 'dp', scatter_dimension=0, tiled=True)]
    dot_general x6 -> x0, matrix products: 24.2 us -> none  [the longest x1 11 us: local_gradients(): lax.dot_general(normed, preact_delta, (((0,), (0,)), ((), ())), preferred...]
    reduce_sum x5 -> x0, other arithmetic: 9.5 us -> none  [the longest x1 2.94 us: local_gradients(): jnp.mean(token_delta * out_normed, axis=1, keepdims=True)]
    reduce_scatter x1, waiting for transfers between devices: 25.6 us -> 31.9 us  [per_device(): lax.psum_scatter(down_term, 'dp', scatter_dimension=0, tiled=True)]
    reshape x2 -> x0, local copies, waits for them, and re-layouts: 5.67 us -> none  [the longest x1 2.87 us: local_gradients(): out_normed.reshape(images, patches, features)]
    all_gather x1, waiting for transfers between devices: 0.01 us -> 5.58 us  [per_device(): down_full = lax.all_gather(down_bf, 'dp', axis=0, tiled=True)]
  transfers between devices with their start and end apart: 4 -> 4, of which waited for: 1 -> 3; matrix products, arithmetic and copies ran while one was open for 14% -> 10% of each run, Pallas kernels for 37% -> 18%
where the time goes in v1:
time: 347 us
  Pallas kernels  200 us (58%)
  waiting for transfers between devices  80.5 us (23%)
  other arithmetic  26.8 us (8%)
  local copies, waits for them, and re-layouts  22.8 us (7%)
  between operations  15.9 us (5%)
    pallas_call x2, Pallas kernels, member_call(): pl.pallas_call(functools.partial(body, n), out_shape=jax.ShapeDtypeStruct...  135 us
    pallas_call x1, Pallas kernels, scatter_with_gradients(): pl.pallas_call(functools.partial(scatter_compute_kernel, n, batch_total,...  65.5 us
    reduce_scatter x1, waiting for transfers between devices, per_device(): up_share = lax.psum_scatter(up_term, 'dp', scatter_dimension=0, tiled=True)  42.4 us
    reduce_scatter x1, waiting for transfers between devices, per_device(): lax.psum_scatter(down_term, 'dp', scatter_dimension=0, tiled=True)  31.9 us
    concatenate x1, other arithmetic, pack_tiles(): jnp.concatenate([lane_major(part.astype(jnp.bfloat16), lanes) for part in...  13.1 us
    broadcast_in_dim x2, other arithmetic, per_device(): return tuple((value[None] for value in up_new + down_new))  10.3 us
  transfers between devices with their start and end apart: 4, of which 3 were waited for; matrix products, arithmetic and copies ran while one was open for 10% of the time, Pallas kernels for 18%

profile of v1, /device:TPU:1, one launch (start us, length us, event | category | flops | bytes accessed | tf_op | source)
XLA Modules:
  0.0 346.8 jit_solution(892707984715704496)
XLA Ops:
  7.2 0.0 copy-start.2
  7.2 0.0 all-gather.3.cloned.1.call-start
  7.2 1.4 convert_element_type.82
  8.6 0.7 convert_element_type.83
  9.4 0.0 copy-done.2
  9.4 0.1 convert_element_type.84
  9.5 0.6 convert_element_type.85
  10.0 0.1 pad.6.clone
  10.1 0.0 copy-start.1
  10.1 0.5 maximum_maximum_fusion.send_ref
  10.6 0.2 copy-done.1
  10.8 72.4 %shard_map.163 = bf16[64,80,128]{2,1,0:T(8,128)(2,1)S(1)} custom-call(s32[64]{0:T(128)S(1)} %copy-done.1, bf16[64,80,128]{2,1,0:T(8,128)(2,1)S(1)} %maximum_maximum_fusion.send_ref), custom_call_target="tpu_custom_call" | custom-call | bytes 26214400 | tf_op jit(solution)/shard_map/pallas_call | solution.py:299
  83.1 0.3 fusion.11
  83.4 1.5 reshape.82
  84.9 0.0 all-gather.3.cloned.1.call-update
  84.9 0.0 all-gather.5.cloned.1.call-start
  85.0 1.4 reshape.83
  86.4 0.0 all-gather.5.cloned.1.call-update
  86.4 0.2 reduce-scatter.5.cloned.1.call-start
  86.6 0.0 copy-done.4
  86.6 0.1 convert_element_type.87
  86.7 0.0 copy-start.9
  86.7 0.4 convert_element_type.88
  87.1 0.2 copy.41
  87.3 0.5 copy-done.9
  87.8 0.4 reshape_squeeze.9
  88.2 0.2 copy.38
  88.3 0.7 copy-done.3
  89.0 0.3 copy.42
  89.3 0.0 copy-start.8
  89.4 0.3 copy.43
  89.7 0.7 copy-done.8
  90.4 0.3 copy.39
  90.7 0.3 copy.40
  91.0 13.1 %pad_maximum_fusion = bf16[9216,128]{1,0:T(8,128)(2,1)S(1)} fusion(bf16[2304,128]{1,0:T(8,128)(2,1)S(1)} %bitcast.98, bf16[2304,128]{1,0:T(8,128)(2,1)S(1)} %bitcast.100, bf16[2304,128]{1,0:T(8,128)(2,1)S(1)} %bitcast.99, bf16[2304,128]{1,0:T(8,128)(2,1)S(1)} %bitcast.101), kind=kLoop, calls=%fused_computation | loop fusion | flops 9437184 | bytes 4718592 | tf_op jit(solution)/shard_map/concatenate | solution.py:360
  104.2 0.0 copy-start.6
  104.2 62.5 %shard_map.164.send_ref = bf16[64,144,128]{2,1,0:T(8,128)(2,1)S(1)} custom-call(s32[64]{0:T(128)S(1)} %copy-done.1, bf16[64,144,128]{2,1,0:T(8,128)(2,1)S(1)} %bitcast.89), custom_call_target="tpu_custom_call" | custom-call | bytes 47185920 | tf_op jit(solution)/shard_map/pallas_call | solution.py:299
  166.7 0.0 copy-start
  166.7 1.5 copy-done
  168.2 0.0 copy-done.6
  168.2 0.1 copy.44
  168.3 0.0 copy-start.7
  168.3 1.2 reshape_squeeze.11.tokens_ref
  169.5 0.1 copy-done.7
  169.6 1.2 copy.45.classifier_ref
  170.8 5.6 %all-gather.5.cloned.1.call-done.down_ref = bf16[1536,768]{1,0:T(8,128)(2,1)} async-done(((bf16[384,768]{1,0:T(8,128)(2,1)}), bf16[1536,768]{1,0:T(8,128)(2,1)}) %all-gather.5.cloned.1.call-update) | async-done | bytes 2359312 | tf_op jit(solution)/shard_map/all_gather | solution.py:397
  176.4 65.5 %shard_map.165 = (bf16[64,144,128]{2,1,0:T(8,128)(2,1)}, bf16[768,1536]{1,0:T(8,128)(2,1)}, bf16[1536,768]{1,0:T(8,128)(2,1)}) custom-call(s32[4]{0:T(128)} %bitcast.106, bf16[64,144,128]{2,1,0:T(8,128)(2,1)} %copy-done, bf16[784,768]{1,0:T(8,128)(2,1)} %reshape_squeeze.11.tokens_ref, bf16[768,1536]{1,0:T(8,128)(2,1)} %all-gather.3.cloned.1.call-done.up_ref, ...), custom_call_target="tpu_custom_call" | custom-call | flops 11098128384 | bytes 47185920 | tf_op jit(solution)/shard_map/pallas_call | solution.py:278
  241.9 0.0 reduce-scatter.5.cloned.1.call-update
  241.9 0.0 reduce-scatter.3.cloned.1.call-start
  241.9 0.5 reduce-scatter.3.cloned.1.call-update
  242.5 0.6 dynamic_slice.3
  245.0 1.4 convert_multiply_fusion.2
  246.4 1.4 copy.48
  247.8 2.7 copy.49
  250.5 2.1 fusion.10
  252.6 0.3 copy.50
  252.9 1.4 copy.51
  254.2 0.7 copy.46
  255.0 0.3 copy-done.5
  255.3 0.4 copy.47
  255.7 31.9 %reduce-scatter.5.cloned.1.call-done = bf16[384,768]{1,0:T(8,128)(2,1)} async-done(((bf16[1536,768]{1,0:T(8,128)(2,1)}), bf16[384,768]{1,0:T(8,128)(2,1)}) %reduce-scatter.5.cloned.1.call-update) | async-done | bytes 589840 | tf_op jit(solution)/shard_map/reduce_scatter | solution.py:407
  287.6 5.0 %fusion.8 = (f32[1,384,768]{2,1,0:T(8,128)}, f32[1,384,768]{2,1,0:T(8,128)}, bf16[1,384,768]{2,1,0:T(8,128)(2,1)}) fusion(bf16[384,768]{1,0:T(8,128)(2,1)} %reduce-scatter.5.cloned.1.call-done, f32[384,768]{1,0:T(8,128)} %copy.51, f32[1,384,768]{2,1,0:T(8,128)} %param.23, pred[]{:T(512)S(6)} %eq.3, f32[]{:T(128)} %bitcast.88, f32[384,768]{1,0:T(8,128)} %copy.49, ...), kind=kLoop, calls=%fused_computation.23 | loop fusion | flops 5308416 | bytes 8847369 | tf_op jit(solution)/shard_map/broadcast_in_dim | solution.py:421
  292.7 42.4 %reduce-scatter.3.cloned.1.call-done = bf16[192,1536]{1,0:T(8,128)(2,1)} async-done(((bf16[768,1536]{1,0:T(8,128)(2,1)}), bf16[192,1536]{1,0:T(8,128)(2,1)}) %reduce-scatter.3.cloned.1.call-update) | async-done | bytes 589840 | tf_op jit(solution)/shard_map/reduce_scatter | solution.py:406
  335.1 5.2 %fusion.9 = (f32[1,192,1536]{2,1,0:T(8,128)}, f32[1,192,1536]{2,1,0:T(8,128)}, bf16[1,192,1536]{2,1,0:T(8,128)(2,1)}) fusion(bf16[192,1536]{1,0:T(8,128)(2,1)} %reduce-scatter.3.cloned.1.call-done, f32[24,8,12,128]{3,2,1,0:T(8,128)S(1)} %bitcast.91, f32[1,192,1536]{2,1,0:T(8,128)} %param.20, pred[]{:T(512)S(6)} %eq.3, f32[]{:T(128)} %bitcast.87, ...), kind=kLoop, calls=%fused_computation.24 | loop fusion | flops 5308416 | bytes 8847369 | tf_op jit(solution)/shard_map/broadcast_in_dim | solution.py:421
  (5 shorter events, 0.0 us)
Async XLA Ops:
  7.2 2.2 copy-start.2
  7.2 163.6 %all-gather.3.cloned.1.call-start = ((), (), s32[]{:S(2)}) async-start(), calls=%async_computation.2 | async-start | bytes 2949120 | tf_op jit(solution)/shard_map/all_gather | solution.py:396
  10.1 0.7 copy-start.1
  84.9 1.7 copy-start.4
  84.9 91.4 %all-gather.5.cloned.1.call-start = ((), (), s32[]{:S(2)}) async-start(), calls=%async_computation.3 | async-start | bytes 2949120 | tf_op jit(solution)/shard_map/all_gather | solution.py:397
  86.4 201.2 %reduce-scatter.5.cloned.1.call-start = ((), (), s32[]{:S(2)}) async-start(), calls=%async_computation.5 | async-start | bytes 2949120 | tf_op jit(solution)/shard_map/reduce_scatter | solution.py:407
  86.7 1.1 copy-start.9
  87.8 1.3 copy-start.3
  89.3 1.1 copy-start.8
  104.2 64.0 %copy-start.6 = (bf16[1,4,196,768]{3,1,2,0:T(4,128)(2,1)S(1)}, bf16[1,4,196,768]{3,1,2,0:T(4,128)(2,1)}, u32[]{:S(2)}) copy-start(bf16[1,4,196,768]{3,1,2,0:T(4,128)(2,1)} %param.12) | copy-start | bytes 3612676
  166.7 1.5 copy-start
  168.3 1.3 copy-start.7
  241.9 93.2 %reduce-scatter.3.cloned.1.call-start = ((), (), s32[]{:S(2)}) async-start(), calls=%async_computation.4 | async-start | bytes 2949120 | tf_op jit(solution)/shard_map/reduce_scatter | solution.py:406
  254.2 1.1 copy-start.5
Sparse Core Ops, SparseCore 0:
  85.1 33.8 all-gather.2
  121.4 54.9 all-gather.4
  242.0 45.5 reduce-scatter.4
  290.5 44.5 reduce-scatter.2

commit v2 on v1

--- a/solution.py
+++ b/solution.py
@@ -233,10 +233,30 @@
 
 def scatter_compute_kernel(
     n, batch_total, patches, labels_ref, send_ref, tokens_ref, up_ref, down_ref, classifier_ref,
-    out_ref, up_grad_ref, down_grad_ref, send_sem, recv_sem,
+    out_ref, up_share_ref, down_share_ref,
+    up_term, down_term, up_near, down_near, up_part, down_part, up_far, down_far,
+    send_sem, recv_sem, near_send, near_recv, far_send, far_recv,
 ):
     me = lax.axis_index("member")
-    enter(n, me)
+    shard = lax.axis_index("dp")
+    core = shard % 2
+    chip = shard // 2
+    partner = chip * 2 + (1 - core)
+    across = (1 - chip) * 2 + core
+    diagonal = (1 - chip) * 2 + (1 - core)
+
+    barrier = pltpu.get_barrier_semaphore()
+
+    def greet(k, carry):
+        pl.semaphore_signal(
+            barrier, inc=1, device_id={"member": lax.rem(me + k, n)}, device_id_type=MESH_ID
+        )
+        return carry
+
+    lax.fori_loop(1, n, greet, 0)
+    for peer in (partner, across, diagonal):
+        pl.semaphore_signal(barrier, inc=1, device_id={"dp": peer}, device_id_type=MESH_ID)
+    pl.semaphore_wait(barrier, n - 1 + 3)
 
     def copy(k):
         target = lax.rem(me + k, n)
@@ -263,8 +283,67 @@
         tokens_ref[...], labels_ref, up_ref[...], down_ref[...], classifier_ref[...],
         batch_total, patches,
     )
-    up_grad_ref[...] = up_gradient.astype(up_grad_ref.dtype)
-    down_grad_ref[...] = down_gradient.astype(down_grad_ref.dtype)
+    up_term[...] = up_gradient.astype(jnp.bfloat16)
+    down_term[...] = down_gradient.astype(jnp.bfloat16)
+
+    def rows(term, index):
+        size = term.shape[0] // 4
+        return term.at[pl.ds(pl.multiple_of(index * size, size), size)]
+
+    near = []
+    slot = 0
+    for term, near_buf in ((up_term, up_near), (down_term, down_near)):
+        for which, index in ((0, diagonal), (1, partner)):
+            near.append(
+                pltpu.make_async_remote_copy(
+                    src_ref=rows(term, index),
+                    dst_ref=near_buf.at[which],
+                    send_sem=near_send.at[slot],
+                    recv_sem=near_recv.at[slot],
+                    device_id={"dp": partner},
+                    device_id_type=MESH_ID,
+                )
+            )
+            slot += 1
+    for item in near:
+        item.start()
+    for item in near:
+        item.wait()
+
+    far = []
+    slot = 0
+    for term, near_buf, part, far_buf in (
+        (up_term, up_near, up_part, up_far),
+        (down_term, down_near, down_part, down_far),
+    ):
+        part[...] = (
+            rows(term, across)[...].astype(jnp.float32) + near_buf[0].astype(jnp.float32)
+        ).astype(jnp.bfloat16)
+        far.append(
+            pltpu.make_async_remote_copy(
+                src_ref=part,
+                dst_ref=far_buf,
+                send_sem=far_send.at[slot],
+                recv_sem=far_recv.at[slot],
+                device_id={"dp": across},
+                device_id_type=MESH_ID,
+            )
+        )
+        slot += 1
+    for item in far:
+        item.start()
+    for item in far:
+        item.wait()
+
+    for term, near_buf, far_buf, share in (
+        (up_term, up_near, up_far, up_share_ref),
+        (down_term, down_near, down_far, down_share_ref),
+    ):
+        share[...] = (
+            rows(term, shard)[...].astype(jnp.float32)
+            + near_buf[1].astype(jnp.float32)
+            + far_buf[...].astype(jnp.float32)
+        )
     lax.fori_loop(1, n, finish, 0)
 
 
@@ -275,16 +354,34 @@
     vmem = pl.BlockSpec(memory_space=pltpu.VMEM)
     moved = picked.size * picked.dtype.itemsize
     flops = 12 * images * patches * features * up_full.shape[1]
+    up_rows = (up_full.shape[0] // 4, up_full.shape[1])
+    down_rows = (down_full.shape[0] // 4, down_full.shape[1])
+    bf16 = jnp.bfloat16
     return pl.pallas_call(
         functools.partial(scatter_compute_kernel, n, batch_total, patches),
         out_shape=(
             jax.ShapeDtypeStruct(picked.shape, picked.dtype),
-            jax.ShapeDtypeStruct(up_full.shape, jnp.bfloat16),
-            jax.ShapeDtypeStruct(down_full.shape, jnp.bfloat16),
+            jax.ShapeDtypeStruct(up_rows, jnp.float32),
+            jax.ShapeDtypeStruct(down_rows, jnp.float32),
         ),
         in_specs=[pl.BlockSpec(memory_space=pltpu.SMEM)] + [vmem] * 5,
         out_specs=(vmem, vmem, vmem),
-        scratch_shapes=[pltpu.SemaphoreType.DMA((n,)), pltpu.SemaphoreType.DMA((n,))],
+        scratch_shapes=[
+            pltpu.VMEM(up_full.shape, bf16),
+            pltpu.VMEM(down_full.shape, bf16),
+            pltpu.VMEM((2,) + up_rows, bf16),
+            pltpu.VMEM((2,) + down_rows, bf16),
+            pltpu.VMEM(up_rows, bf16),
+            pltpu.VMEM(down_rows, bf16),
+            pltpu.VMEM(up_rows, bf16),
+            pltpu.VMEM(down_rows, bf16),
+            pltpu.SemaphoreType.DMA((n,)),
+            pltpu.SemaphoreType.DMA((n,)),
+            pltpu.SemaphoreType.DMA((4,)),
+            pltpu.SemaphoreType.DMA((4,)),
+            pltpu.SemaphoreType.DMA((2,)),
+            pltpu.SemaphoreType.DMA((2,)),
+        ],
         compiler_params=pltpu.CompilerParams(
             collective_id=kernel_id, has_side_effects=True, vmem_limit_bytes=63 * 1024 * 1024
         ),
@@ -400,14 +497,10 @@
     up_full, down_full, picked = lax.optimization_barrier((up_full, down_full, picked))
 
     batch_total = tokens.shape[1] * shards
-    back, up_term, down_term = scatter_with_gradients(
+    back, up_share, down_share = scatter_with_gradients(
         picked, tokens[0], labels[0], up_full, down_full, classifier, batch_total, 2
     )
-    up_share = lax.psum_scatter(up_term, "dp", scatter_dimension=0, tiled=True)
-    down_share = lax.psum_scatter(down_term, "dp", scatter_dimension=0, tiled=True)
     up_mom, down_mom, up_var_bf, down_var_bf = unpack_tiles(back, moments)
-    up_share = up_share.astype(jnp.float32)
-    down_share = down_share.astype(jnp.float32)
 
     up_now = jnp.where(own, up_param[0], up_bf.astype(jnp.float32))
     down_now = jnp.where(own, down_param[0], down_bf.astype(jnp.float32))

time: 347 us -> 285 us (0.82)
  waiting for transfers between devices: 80.5 us -> 3.26 us
  Pallas kernels: 200 us -> 217 us
  other arithmetic: 26.8 us -> 22.5 us
    reduce_scatter x2 -> x0, waiting for transfers between devices: 74.4 us -> none  [the longest x1 42.4 us: per_device(): up_share = lax.psum_scatter(up_term, 'dp', scatter_dimension=0, tiled=True)]
    pallas_call x1, Pallas kernels: 65.5 us -> 82 us  [scatter_with_gradients(): pl.pallas_call(functools.partial(scatter_compute_kernel, n, batch_total,...]
    broadcast_in_dim x2, other arithmetic: 10.3 us -> 5.77 us  [per_device(): return tuple((value[None] for value in up_new + down_new))]
  transfers between devices with their start and end apart: 4 -> 2, of which waited for: 3 -> 1; matrix products, arithmetic and copies ran while one was open for 10% -> 8% of each run, Pallas kernels for 18% -> 22%
where the time goes in v2:
time: 285 us; the launch traced here: 282 us
  Pallas kernels  217 us (76%)
  other arithmetic  22.5 us (8%)
  local copies, waits for them, and re-layouts  22 us (8%)
  between operations  16.5 us (6%)
  waiting for transfers between devices  3.26 us (1%)
    pallas_call x2, Pallas kernels, member_call(): pl.pallas_call(functools.partial(body, n), out_shape=jax.ShapeDtypeStruct...  135 us
    pallas_call x1, Pallas kernels, scatter_with_gradients(): pl.pallas_call(functools.partial(scatter_compute_kernel, n, batch_total,...  82 us
    concatenate x1, other arithmetic, pack_tiles(): jnp.concatenate([lane_major(part.astype(jnp.bfloat16), lanes) for part in...  13.1 us
    unnamed x40, local copies, waits for them, and re-layouts  5.86 us
    broadcast_in_dim x2, other arithmetic, per_device(): return tuple((value[None] for value in up_new + down_new))  5.77 us
  transfers between devices with their start and end apart: 2, of which 1 were waited for; matrix products, arithmetic and copies ran while one was open for 8% of the time, Pallas kernels for 22%

profile of v2, /device:TPU:1, one launch (start us, length us, event | category | flops | bytes accessed | tf_op | source)
XLA Modules:
  0.0 281.5 jit_solution(7461333036843230068)
XLA Ops:
  7.2 0.0 copy-start.6
  7.2 0.0 all-gather.3.cloned.1.call-start
  7.2 1.4 convert_element_type.76
  8.6 0.7 convert_element_type.77
  9.4 0.0 copy-done.6
  9.4 0.1 convert_element_type.78
  9.5 0.6 convert_element_type.79
  10.0 0.1 pad.6.clone
  10.1 0.5 maximum_maximum_fusion.send_ref
  10.6 0.2 copy-done.1
  10.8 72.4 %shard_map.163 = bf16[64,80,128]{2,1,0:T(8,128)(2,1)S(1)} custom-call(s32[64]{0:T(128)S(1)} %copy-done.1, bf16[64,80,128]{2,1,0:T(8,128)(2,1)S(1)} %maximum_maximum_fusion.send_ref), custom_call_target="tpu_custom_call" | custom-call | bytes 26214400 | tf_op jit(solution)/shard_map/pallas_call | solution.py:396
  83.1 0.3 fusion.7
  83.4 1.5 reshape.82
  84.9 0.0 all-gather.3.cloned.1.call-update
  84.9 0.3 all-gather.5.cloned.1.call-start
  85.2 1.4 reshape.83
  86.6 0.0 all-gather.5.cloned.1.call-update
  86.6 0.1 convert_element_type.81
  86.7 0.4 convert_element_type.82
  87.1 0.2 copy.41
  87.3 0.0 copy-start.4
  87.3 1.6 reshape_squeeze.9
  88.9 0.2 copy.38
  89.1 0.0 copy-start.17
  89.1 0.3 copy.42
  89.4 0.3 copy.43
  89.8 0.4 copy-done.17
  90.2 0.3 copy.39
  90.5 0.3 copy.40
  90.8 13.1 %pad_maximum_fusion = bf16[9216,128]{1,0:T(8,128)(2,1)S(1)} fusion(bf16[2304,128]{1,0:T(8,128)(2,1)S(1)} %bitcast.98, bf16[2304,128]{1,0:T(8,128)(2,1)S(1)} %bitcast.100, bf16[2304,128]{1,0:T(8,128)(2,1)S(1)} %bitcast.99, bf16[2304,128]{1,0:T(8,128)(2,1)S(1)} %bitcast.101), kind=kLoop, calls=%fused_computation | loop fusion | flops 9437184 | bytes 4718592 | tf_op jit(solution)/shard_map/concatenate | solution.py:457
  103.9 0.0 copy-start.13
  103.9 62.5 %shard_map.164.send_ref = bf16[64,144,128]{2,1,0:T(8,128)(2,1)S(1)} custom-call(s32[64]{0:T(128)S(1)} %copy-done.1, bf16[64,144,128]{2,1,0:T(8,128)(2,1)S(1)} %bitcast.89), custom_call_target="tpu_custom_call" | custom-call | bytes 47185920 | tf_op jit(solution)/shard_map/pallas_call | solution.py:396
  166.5 0.0 copy-start
  166.5 1.4 copy-done
  167.9 0.1 copy.44
  168.1 0.0 copy-start.16
  168.1 1.2 reshape_squeeze.11.tokens_ref
  169.3 0.1 copy-done.16
  169.4 1.2 copy.45.classifier_ref
  170.5 0.6 dynamic_slice.3
  173.1 0.0 all-gather.3.cloned.1.call-done.up_ref
  173.1 3.2 %all-gather.5.cloned.1.call-done.down_ref = bf16[1536,768]{1,0:T(8,128)(2,1)} async-done(((bf16[384,768]{1,0:T(8,128)(2,1)}), bf16[1536,768]{1,0:T(8,128)(2,1)}) %all-gather.5.cloned.1.call-update) | async-done | bytes 2359312 | tf_op jit(solution)/shard_map/all_gather | solution.py:494
  176.3 82.0 %shard_map.165 = (bf16[64,144,128]{2,1,0:T(8,128)(2,1)}, f32[192,1536]{1,0:T(8,128)}, f32[384,768]{1,0:T(8,128)}) custom-call(s32[4]{0:T(128)} %bitcast.106, bf16[64,144,128]{2,1,0:T(8,128)(2,1)} %copy-done, bf16[784,768]{1,0:T(8,128)(2,1)} %reshape_squeeze.11.tokens_ref, bf16[768,1536]{1,0:T(8,128)(2,1)} %all-gather.3.cloned.1.call-done.up_ref, ...), custom_call_target="tpu_custom_call" | custom-call | flops 11098128384 | bytes 47185920 | tf_op jit(solution)/shard_map/pallas_call | solution.py:360
  258.3 0.0 copy-start.11
  258.4 1.6 convert_multiply_fusion
  259.9 0.4 copy-done.11
  260.4 1.1 fusion.6
  261.4 0.4 copy.48
  261.8 0.4 copy.49
  262.2 2.3 copy.50
  264.5 1.6 copy.51
  266.2 0.0 copy-start.12
  266.2 0.0 copy-start.7
  266.2 0.7 copy.46
  266.9 0.0 copy-start.2
  266.9 0.0 copy-start.5
  266.9 0.3 copy-done.12
  267.2 0.4 copy.47
  267.6 0.0 copy-done.7
  267.6 0.4 copy-done.14
  268.0 0.3 copy-done.2
  268.3 0.4 copy-done.5
  268.7 2.7 fusion.4
  271.4 3.1 %fusion.5 = (f32[1,192,1536]{2,1,0:T(8,128)}, f32[1,192,1536]{2,1,0:T(8,128)}, bf16[1,192,1536]{2,1,0:T(8,128)(2,1)}) fusion(f32[192,1536]{1,0:T(8,128)S(1)} %copy-done.15, f32[24,8,12,128]{3,2,1,0:T(8,128)S(1)} %bitcast.91, f32[1,192,1536]{2,1,0:T(8,128)S(1)} %copy-done.9, pred[]{:T(512)S(6)} %eq.3, f32[]{:T(128)} %bitcast.87, ...), kind=kLoop, calls=%fused_computation.21 | loop fusion | flops 5013504 | bytes 9437193 | tf_op jit(solution)/shard_map/broadcast_in_dim | solution.py:514
  (15 shorter events, 0.0 us)
Async XLA Ops:
  7.2 2.2 copy-start.6
  7.2 165.9 %all-gather.3.cloned.1.call-start = ((), (), s32[]{:S(2)}) async-start(), calls=%async_computation | async-start | bytes 2949120 | tf_op jit(solution)/shard_map/all_gather | solution.py:493
  10.1 0.7 copy-start.1
  84.9 1.7 copy-start.8
  84.9 91.4 %all-gather.5.cloned.1.call-start = ((), (), s32[]{:S(2)}) async-start(), calls=%async_computation.1 | async-start | bytes 2949120 | tf_op jit(solution)/shard_map/all_gather | solution.py:494
  87.3 1.8 copy-start.4
  89.1 1.1 copy-start.17
  103.9 64.0 %copy-start.13 = (bf16[1,4,196,768]{3,1,2,0:T(4,128)(2,1)S(1)}, bf16[1,4,196,768]{3,1,2,0:T(4,128)(2,1)}, u32[]{:S(2)}) copy-start(bf16[1,4,196,768]{3,1,2,0:T(4,128)(2,1)} %param.12) | copy-start | bytes 3612676
  166.5 1.4 copy-start
  168.1 1.3 copy-start.16
  258.3 2.0 copy-start.11
  266.2 1.1 copy-start.12
  266.2 1.4 copy-start.7
  266.2 1.8 copy-start.14
  266.9 1.4 copy-start.2
  266.9 1.8 copy-start.5
  268.7 2.7 copy-start.3
  268.7 2.7 copy-start.9
  268.7 2.7 copy-start.10
  268.7 2.7 copy-start.15
Sparse Core Ops, SparseCore 0:
  85.0 34.0 all-gather.2
  121.5 54.7 all-gather.4

commit v3 on v2

--- a/solution.py
+++ b/solution.py
@@ -142,10 +142,41 @@
     transpose(n, me, picked, out_ref, send2, recv2)
 
 
-def gather_kernel(n, source_ref, send_ref, out_ref, held, send1, recv1):
+def gather_kernel(n, source_ref, *refs):
+    parts, (out_ref, flat, held, send1, recv1) = refs[:-5], refs[-5:]
     me = lax.axis_index("member")
+    lanes = flat.shape[1]
+    chunk = held.shape[1]
+    offset = 0
+    for part in parts:
+        rows, cols = part.shape
+        for block in range(cols // lanes):
+            flat[pl.ds(offset, rows), :] = part[:, pl.ds(block * lanes, lanes)].astype(flat.dtype)
+            offset += rows
     enter(n, me)
-    transpose(n, me, send_ref, held, send1, recv1)
+
+    def copy(k):
+        target = lax.rem(me + k, n)
+        return pltpu.make_async_remote_copy(
+            src_ref=flat.at[pl.ds(pl.multiple_of(target * chunk, 16), chunk)],
+            dst_ref=held.at[me],
+            send_sem=send1.at[k],
+            recv_sem=recv1.at[k],
+            device_id={"member": target},
+            device_id_type=MESH_ID,
+        )
+
+    def start(k, carry):
+        copy(k).start()
+        return carry
+
+    def finish(k, carry):
+        copy(k).wait()
+        return carry
+
+    lax.fori_loop(1, n, start, 0)
+    held[me] = flat[pl.ds(pl.multiple_of(me * chunk, 16), chunk)]
+    lax.fori_loop(1, n, finish, 0)
     pick_rows(n, source_ref, held, out_ref)
 
 
@@ -233,8 +264,8 @@
 
 def scatter_compute_kernel(
     n, batch_total, patches, labels_ref, send_ref, tokens_ref, up_ref, down_ref, classifier_ref,
-    out_ref, up_share_ref, down_share_ref,
-    up_term, down_term, up_near, down_near, up_part, down_part, up_far, down_far,
+    up_share_ref, down_share_ref, up_first_ref, down_first_ref, up_second_ref, down_second_ref,
+    flat, up_term, down_term, up_near, down_near, up_part, down_part, up_far, down_far,
     send_sem, recv_sem, near_send, near_recv, far_send, far_recv,
 ):
     me = lax.axis_index("member")
@@ -258,11 +289,13 @@
         pl.semaphore_signal(barrier, inc=1, device_id={"dp": peer}, device_id_type=MESH_ID)
     pl.semaphore_wait(barrier, n - 1 + 3)
 
+    chunk = send_ref.shape[1]
+
     def copy(k):
         target = lax.rem(me + k, n)
         return pltpu.make_async_remote_copy(
             src_ref=send_ref.at[target],
-            dst_ref=out_ref.at[me],
+            dst_ref=flat.at[pl.ds(pl.multiple_of(me * chunk, 16), chunk)],
             send_sem=send_sem.at[k],
             recv_sem=recv_sem.at[k],
             device_id={"member": target},
@@ -278,7 +311,7 @@
         return carry
 
     lax.fori_loop(1, n, start, 0)
-    out_ref[me] = send_ref[me]
+    flat[pl.ds(pl.multiple_of(me * chunk, 16), chunk)] = send_ref[me]
     up_gradient, down_gradient = block_gradients(
         tokens_ref[...], labels_ref, up_ref[...], down_ref[...], classifier_ref[...],
         batch_total, patches,
@@ -345,6 +378,13 @@
             + far_buf[...].astype(jnp.float32)
         )
     lax.fori_loop(1, n, finish, 0)
+    lanes = flat.shape[1]
+    offset = 0
+    for part in (up_first_ref, down_first_ref, up_second_ref, down_second_ref):
+        rows, cols = part.shape
+        for block in range(cols // lanes):
+            part[:, pl.ds(block * lanes, lanes)] = flat[pl.ds(offset, rows), :]
+            offset += rows
 
 
 def scatter_with_gradients(picked, tokens, labels, up_full, down_full, classifier, batch_total,
@@ -360,13 +400,13 @@
     return pl.pallas_call(
         functools.partial(scatter_compute_kernel, n, batch_total, patches),
         out_shape=(
-            jax.ShapeDtypeStruct(picked.shape, picked.dtype),
             jax.ShapeDtypeStruct(up_rows, jnp.float32),
             jax.ShapeDtypeStruct(down_rows, jnp.float32),
-        ),
+        ) + tuple(jax.ShapeDtypeStruct(shape, bf16) for shape in (up_rows, down_rows) * 2),
         in_specs=[pl.BlockSpec(memory_space=pltpu.SMEM)] + [vmem] * 5,
-        out_specs=(vmem, vmem, vmem),
+        out_specs=(vmem,) * 6,
         scratch_shapes=[
+            pltpu.VMEM((picked.shape[0] * picked.shape[1], picked.shape[2]), bf16),
             pltpu.VMEM(up_full.shape, bf16),
             pltpu.VMEM(down_full.shape, bf16),
             pltpu.VMEM((2,) + up_rows, bf16),
@@ -413,11 +453,28 @@
     return member_call(exploit_kernel, packed, (source, packed), [block, block] + sems, kernel_id)
 
 
-def exploit_gather(packed, source, kernel_id):
-    n, rows, lanes = packed.shape
-    block = pltpu.VMEM((n, rows, lanes), packed.dtype)
-    sems = [pltpu.SemaphoreType.DMA((n,))] * 2
-    return member_call(gather_kernel, packed, (source, packed), [block] + sems, kernel_id)
+def exploit_gather(parts, source, members, kernel_id):
+    lanes = 128
+    total = sum(part.size for part in parts) // lanes
+    shape = (members, total // members, lanes)
+    vmem = pl.BlockSpec(memory_space=pltpu.VMEM)
+    moved = total * lanes * 2
+    return pl.pallas_call(
+        functools.partial(gather_kernel, members),
+        out_shape=jax.ShapeDtypeStruct(shape, jnp.bfloat16),
+        in_specs=[pl.BlockSpec(memory_space=pltpu.SMEM)] + [vmem] * len(parts),
+        out_specs=vmem,
+        scratch_shapes=[
+            pltpu.VMEM((total, lanes), jnp.bfloat16),
+            pltpu.VMEM(shape, jnp.bfloat16),
+            pltpu.SemaphoreType.DMA((members,)),
+            pltpu.SemaphoreType.DMA((members,)),
+        ],
+        compiler_params=pltpu.CompilerParams(
+            collective_id=kernel_id, has_side_effects=True, vmem_limit_bytes=48 * 1024 * 1024
+        ),
+        cost_estimate=pl.CostEstimate(flops=0, transcendentals=0, bytes_accessed=moved * 20),
+    )(source, *parts)
 
 
 def exploit_scatter(packed, kernel_id):
@@ -493,14 +550,13 @@
     up_full = lax.all_gather(up_bf, "dp", axis=0, tiled=True)
     down_full = lax.all_gather(down_bf, "dp", axis=0, tiled=True)
     moments = (up_first[0], down_first[0], up_second[0], down_second[0])
-    picked = exploit_gather(pack_tiles(moments, members), source, 1)
+    picked = exploit_gather(moments, source, members, 1)
     up_full, down_full, picked = lax.optimization_barrier((up_full, down_full, picked))
 
     batch_total = tokens.shape[1] * shards
-    back, up_share, down_share = scatter_with_gradients(
+    up_share, down_share, up_mom, down_mom, up_var_bf, down_var_bf = scatter_with_gradients(
         picked, tokens[0], labels[0], up_full, down_full, classifier, batch_total, 2
     )
-    up_mom, down_mom, up_var_bf, down_var_bf = unpack_tiles(back, moments)
 
     up_now = jnp.where(own, up_param[0], up_bf.astype(jnp.float32))
     down_now = jnp.where(own, down_param[0], down_bf.astype(jnp.float32))

time: 285 us -> 267 us (0.937); the launches traced: 282 us -> 267 us
  other arithmetic: 22.5 us -> 10.1 us
  waiting for transfers between devices: 3.26 us -> 14.7 us
  local copies, waits for them, and re-layouts: 22 us -> 12.7 us
  Pallas kernels: 217 us -> 213 us
    pallas_call x0 -> x1, Pallas kernels: none -> 62.9 us  [exploit_gather(): pl.pallas_call(functools.partial(gather_kernel, members), out_shape=jax.S...]
    pallas_call x2 -> x1, Pallas kernels: 135 us -> 72.4 us  [member_call(): pl.pallas_call(functools.partial(body, n), out_shape=jax.ShapeDtypeStruct...]
    concatenate x1 -> x0, other arithmetic: 13.1 us -> none  [pack_tiles(): jnp.concatenate([lane_major(part.astype(jnp.bfloat16), lanes) for part in...]
    all_gather x1, waiting for transfers between devices: 3.21 us -> 14.6 us  [per_device(): down_full = lax.all_gather(down_bf, 'dp', axis=0, tiled=True)]
    convert_element_type x4 -> x0, local copies, waits for them, and re-layouts: 4.72 us -> none  [the longest x2 3.95 us: per_device(): down_var = jnp.where(own, down_second[0], down_var_bf.astype(jnp.float32))]
    pallas_call x1, Pallas kernels: 82 us -> 78.2 us  [scatter_with_gradients(): pl.pallas_call(functools.partial(scatter_compute_kernel, n, batch_total,...]
    unnamed x40 -> x32, local copies, waits for them, and re-layouts: 5.86 us -> 5.19 us
  transfers between devices with their start and end apart: 2 -> 2, of which waited for: 1 -> 1; matrix products, arithmetic and copies ran while one was open for 8% -> 3% of each run, Pallas kernels for 22% -> 24%
where the time goes in v3:
time: 267 us
  Pallas kernels  213 us (80%)
  between operations  16.2 us (6%)
  waiting for transfers between devices  14.7 us (6%)
  local copies, waits for them, and re-layouts  12.7 us (5%)
  other arithmetic  10.1 us (4%)
    pallas_call x1, Pallas kernels, scatter_with_gradients(): pl.pallas_call(functools.partial(scatter_compute_kernel, n, batch_total,...  78.2 us
    pallas_call x1, Pallas kernels, member_call(): pl.pallas_call(functools.partial(body, n), out_shape=jax.ShapeDtypeStruct...  72.4 us
    pallas_call x1, Pallas kernels, exploit_gather(): pl.pallas_call(functools.partial(gather_kernel, members), out_shape=jax.S...  62.9 us
    all_gather x1, waiting for transfers between devices, per_device(): down_full = lax.all_gather(down_bf, 'dp', axis=0, tiled=True)  14.6 us
    broadcast_in_dim x2, other arithmetic, per_device(): return tuple((value[None] for value in up_new + down_new))  8.08 us
  transfers between devices with their start and end apart: 2, of which 1 were waited for; matrix products, arithmetic and copies ran while one was open for 3% of the time, Pallas kernels for 24%

profile of v3, /device:TPU:1, one launch (start us, length us, event | category | flops | bytes accessed | tf_op | source)
XLA Modules:
  0.0 267.2 jit_solution(2872121459578167601)
XLA Ops:
  7.2 0.0 copy-start.9
  7.2 0.0 all-gather.3.cloned.1.call-start
  7.2 1.4 convert_element_type.38
  8.6 0.7 convert_element_type.39
  9.4 0.0 copy-done.9
  9.4 0.1 convert_element_type.40
  9.5 0.6 convert_element_type.41
  10.0 0.1 pad.2.clone
  10.1 0.0 copy-start.6
  10.1 0.5 maximum_maximum_fusion.send_ref
  10.6 0.2 copy-done.6
  10.8 72.4 %shard_map.163 = bf16[64,80,128]{2,1,0:T(8,128)(2,1)S(1)} custom-call(s32[64]{0:T(128)S(1)} %copy-done.6, bf16[64,80,128]{2,1,0:T(8,128)(2,1)S(1)} %maximum_maximum_fusion.send_ref), custom_call_target="tpu_custom_call" | custom-call | bytes 26214400 | tf_op jit(solution)/shard_map/pallas_call | solution.py:436
  83.1 0.3 fusion.8
  83.4 1.5 reshape.24
  84.9 0.0 copy-start.11
  84.9 0.0 all-gather.3.cloned.1.call-update
  84.9 0.0 all-gather.5.cloned.1.call-start
  85.0 1.4 reshape.25
  86.4 0.0 all-gather.5.cloned.1.call-update
  86.4 0.0 copy-done.11
  86.4 1.2 copy.20
  87.6 0.0 copy-start.1
  87.6 0.0 copy-start.4
  87.6 0.0 copy-start.5
  87.6 2.4 reshape_squeeze.3.tokens_ref
  90.0 0.0 copy-start
  90.0 2.4 copy.21.classifier_ref
  92.4 0.6 dynamic_slice.3
  94.9 0.0 copy-done.1
  94.9 0.0 copy-done.4
  95.0 0.0 copy-done.5
  95.0 0.0 copy-done
  95.0 62.9 %shard_map.164.send_ref = bf16[64,144,128]{2,1,0:T(8,128)(2,1)S(1)} custom-call(s32[64]{0:T(128)S(1)} %copy-done.6, bf16[192,1536]{1,0:T(8,128)(2,1)S(1)} %bitcast.38, bf16[384,768]{1,0:T(8,128)(2,1)S(1)} %bitcast.39, f32[192,1536]{1,0:T(8,128)S(1)} %bitcast.37, f32[384,768]{1,0:T(8,128)S(1)} %bitcast.36), custom_call_target="tpu_custom_call" | custom-call | bytes 47185920 | tf_op jit(solution)/shard_map/pallas_call | solution.py:462
  157.9 0.0 copy-start.3
  157.9 1.4 copy-done.3
  159.3 0.0 all-gather.3.cloned.1.call-done.up_ref
  159.3 14.6 %all-gather.5.cloned.1.call-done.down_ref = bf16[1536,768]{1,0:T(8,128)(2,1)} async-done(((bf16[384,768]{1,0:T(8,128)(2,1)}), bf16[1536,768]{1,0:T(8,128)(2,1)}) %all-gather.5.cloned.1.call-update) | async-done | bytes 2359312 | tf_op jit(solution)/shard_map/all_gather | solution.py:551
  173.9 0.0 copy-start.8
  173.9 78.2 %shard_map.165 = (f32[192,1536]{1,0:T(8,128)}, f32[384,768]{1,0:T(8,128)}, bf16[192,1536]{1,0:T(8,128)(2,1)}, bf16[384,768]{1,0:T(8,128)(2,1)}, bf16[192,1536]{1,0:T(8,128)(2,1)}, /*index=5*/bf16[384,768]{1,0:T(8,128)(2,1)}) custom-call(s32[4]{0:T(128)} %bitcast.40, bf16[64,144,128]{2,1,0:T(8,128)(2,1)} %copy-done.3, ...), custom_call_target="tpu_custom_call" | custom-call | flops 11098128384 | bytes 47185920 | tf_op jit(solution)/shard_map/pallas_call | solution.py:400
  252.2 0.0 copy-done.8
  252.2 0.0 copy-start.2
  252.2 0.0 copy-start.7
  252.2 0.0 copy-start.10
  252.2 0.0 copy-start.12
  252.2 0.0 copy-start.13
  252.2 0.0 copy-start.14
  252.2 5.3 %fusion.6 = (f32[1,384,768]{2,1,0:T(8,128)}, f32[1,384,768]{2,1,0:T(8,128)}, bf16[1,384,768]{2,1,0:T(8,128)(2,1)}) fusion(f32[384,768]{1,0:T(8,128)} %get-tuple-element.22, bf16[384,768]{1,0:T(8,128)(2,1)} %get-tuple-element.23, pred[]{:T(512)S(6)} %eq.3, f32[1,384,768]{2,1,0:T(8,128)} %param.23, f32[]{:T(128)} %bitcast.35, ...), kind=kLoop, calls=%fused_computation.15 | loop fusion | flops 5898240 | bytes 8257545 | tf_op jit(solution)/shard_map/broadcast_in_dim | solution.py:570
  257.5 0.0 copy-done.2
  257.6 0.0 copy-done.7
  257.6 0.0 copy-done.10
  257.6 0.0 copy-done.12
  257.6 0.0 copy-done.13
  257.6 0.0 copy-done.14
  257.6 2.8 %fusion.7 = (f32[1,192,1536]{2,1,0:T(8,128)}, f32[1,192,1536]{2,1,0:T(8,128)}, bf16[1,192,1536]{2,1,0:T(8,128)(2,1)}) fusion(f32[192,1536]{1,0:T(8,128)S(1)} %copy-done.12, bf16[192,1536]{1,0:T(8,128)(2,1)S(1)} %copy-done.14, pred[]{:T(512)S(6)} %eq.3, f32[1,192,1536]{2,1,0:T(8,128)S(1)} %copy-done.2, f32[]{:T(128)} %bitcast.34, ...), kind=kLoop, calls=%fused_computation.16 | loop fusion | flops 5898240 | bytes 8257545 | tf_op jit(solution)/shard_map/broadcast_in_dim | solution.py:570
  (1 shorter events, 0.0 us)
Async XLA Ops:
  7.2 2.2 copy-start.9
  7.2 152.1 %all-gather.3.cloned.1.call-start = ((), (), s32[]{:S(2)}) async-start(), calls=%async_computation | async-start | bytes 2949120 | tf_op jit(solution)/shard_map/all_gather | solution.py:550
  10.1 0.7 copy-start.6
  84.9 1.5 copy-start.11
  84.9 89.0 %all-gather.5.cloned.1.call-start = ((), (), s32[]{:S(2)}) async-start(), calls=%async_computation.1 | async-start | bytes 2949120 | tf_op jit(solution)/shard_map/all_gather | solution.py:551
  87.6 7.4 %copy-start.1 = (f32[1,192,1536]{2,1,0:T(8,128)S(1)}, f32[1,192,1536]{2,1,0:T(8,128)}, u32[]{:S(2)}) copy-start(f32[1,192,1536]{2,1,0:T(8,128)} %param.20) | copy-start | bytes 3538948
  87.6 7.4 %copy-start.4 = (bf16[1,192,1536]{2,1,0:T(8,128)(2,1)S(1)}, bf16[1,192,1536]{2,1,0:T(8,128)(2,1)}, u32[]{:S(2)}) copy-start(bf16[1,192,1536]{2,1,0:T(8,128)(2,1)} %param.19) | copy-start | bytes 1769476
  87.6 7.4 %copy-start.5 = (bf16[1,384,768]{2,1,0:T(8,128)(2,1)S(1)}, bf16[1,384,768]{2,1,0:T(8,128)(2,1)}, u32[]{:S(2)}) copy-start(bf16[1,384,768]{2,1,0:T(8,128)(2,1)} %param.22) | copy-start | bytes 1769476
  90.0 4.9 %copy-start = (f32[1,384,768]{2,1,0:T(8,128)S(1)}, f32[1,384,768]{2,1,0:T(8,128)}, u32[]{:S(2)}) copy-start(f32[1,384,768]{2,1,0:T(8,128)} %param.23) | copy-start | bytes 3538948
  157.9 1.4 copy-start.3
  173.9 78.2 %copy-start.8 = (bf16[384,768]{1,0:T(8,128)(2,1)S(1)}, bf16[384,768]{1,0:T(8,128)(2,1)}, u32[]{:S(2)}) copy-start(bf16[384,768]{1,0:T(8,128)(2,1)} %reshape.25) | copy-start | bytes 1769476
  252.2 5.4 %copy-start.2 = (f32[1,192,1536]{2,1,0:T(8,128)S(1)}, f32[1,192,1536]{2,1,0:T(8,128)}, u32[]{:S(2)}) copy-start(f32[1,192,1536]{2,1,0:T(8,128)} %param.20) | copy-start | bytes 3538948
  252.2 5.4 %copy-start.7 = (bf16[192,1536]{1,0:T(8,128)(2,1)S(1)}, bf16[192,1536]{1,0:T(8,128)(2,1)}, u32[]{:S(2)}) copy-start(bf16[192,1536]{1,0:T(8,128)(2,1)} %reshape.24) | copy-start | bytes 1769476
  252.2 5.4 %copy-start.10 = (f32[1,192,1536]{2,1,0:T(8,128)S(1)}, f32[1,192,1536]{2,1,0:T(8,128)}, u32[]{:S(2)}) copy-start(f32[1,192,1536]{2,1,0:T(8,128)} %param.18) | copy-start | bytes 3538948
  252.2 5.3 %copy-start.12 = (f32[192,1536]{1,0:T(8,128)S(1)}, f32[192,1536]{1,0:T(8,128)}, u32[]{:S(2)}) copy-start(f32[192,1536]{1,0:T(8,128)} %get-tuple-element.19) | copy-start | bytes 3538948
  252.2 5.3 %copy-start.13 = (bf16[192,1536]{1,0:T(8,128)(2,1)S(1)}, bf16[192,1536]{1,0:T(8,128)(2,1)}, u32[]{:S(2)}) copy-start(bf16[192,1536]{1,0:T(8,128)(2,1)} %get-tuple-element.18) | copy-start | bytes 1769476
  252.2 5.3 %copy-start.14 = (bf16[192,1536]{1,0:T(8,128)(2,1)S(1)}, bf16[192,1536]{1,0:T(8,128)(2,1)}, u32[]{:S(2)}) copy-start(bf16[192,1536]{1,0:T(8,128)(2,1)} %get-tuple-element.20) | copy-start | bytes 1769476
Sparse Core Ops, SparseCore 0:
  85.1 42.1 all-gather.2
  129.7 44.2 all-gather.4

commit v4 on v3

--- a/solution.py
+++ b/solution.py
@@ -142,9 +142,16 @@
     transpose(n, me, picked, out_ref, send2, recv2)
 
 
-def gather_kernel(n, source_ref, *refs):
-    parts, (out_ref, flat, held, send1, recv1) = refs[:-5], refs[-5:]
+def gather_kernel(n, source_ref, up_ref, down_ref, *refs):
+    parts = refs[:-13]
+    (out_ref, up_full, down_full, flat, held, send1, recv1,
+     near_send, near_recv, far_send, far_recv, fwd_send, fwd_recv) = refs[-13:]
     me = lax.axis_index("member")
+    shard = lax.axis_index("dp")
+    core = shard % 2
+    chip = shard // 2
+    partner = chip * 2 + (1 - core)
+    across = (1 - chip) * 2 + core
     lanes = flat.shape[1]
     chunk = held.shape[1]
     offset = 0
@@ -153,7 +160,37 @@
         for block in range(cols // lanes):
             flat[pl.ds(offset, rows), :] = part[:, pl.ds(block * lanes, lanes)].astype(flat.dtype)
             offset += rows
-    enter(n, me)
+
+    barrier = pltpu.get_barrier_semaphore()
+
+    def greet(k, carry):
+        pl.semaphore_signal(
+            barrier, inc=1, device_id={"member": lax.rem(me + k, n)}, device_id_type=MESH_ID
+        )
+        return carry
+
+    lax.fori_loop(1, n, greet, 0)
+    for peer in (partner, across):
+        pl.semaphore_signal(barrier, inc=1, device_id={"dp": peer}, device_id_type=MESH_ID)
+    pl.semaphore_wait(barrier, n - 1 + 2)
+
+    def rows_of(full, index):
+        size = full.shape[0] // 4
+        return full.at[pl.ds(pl.multiple_of(index * size, size), size)]
+
+    def dp_copy(src, dst, send, recv, slot, peer):
+        return pltpu.make_async_remote_copy(
+            src_ref=src, dst_ref=dst, send_sem=send.at[slot], recv_sem=recv.at[slot],
+            device_id={"dp": peer}, device_id_type=MESH_ID,
+        )
+
+    shares = ((up_ref, up_full), (down_ref, down_full))
+    far = [dp_copy(share, rows_of(full, shard), far_send, far_recv, slot, across)
+           for slot, (share, full) in enumerate(shares)]
+    near = [dp_copy(share, rows_of(full, shard), near_send, near_recv, slot, partner)
+            for slot, (share, full) in enumerate(shares)]
+    for item in far + near:
+        item.start()
 
     def copy(k):
         target = lax.rem(me + k, n)
@@ -176,8 +213,19 @@
 
     lax.fori_loop(1, n, start, 0)
     held[me] = flat[pl.ds(pl.multiple_of(me * chunk, 16), chunk)]
+    for share, full in shares:
+        rows_of(full, shard)[...] = share[...]
+    for item in far:
+        item.wait()
+    forward = [dp_copy(rows_of(full, across), rows_of(full, across), fwd_send, fwd_recv, slot,
+                       partner)
+               for slot, (share, full) in enumerate(shares)]
+    for item in forward:
+        item.start()
     lax.fori_loop(1, n, finish, 0)
     pick_rows(n, source_ref, held, out_ref)
+    for item in near + forward:
+        item.wait()
 
 
 def scatter_kernel(n, send_ref, out_ref, send1, recv1):
@@ -453,28 +501,31 @@
     return member_call(exploit_kernel, packed, (source, packed), [block, block] + sems, kernel_id)
 
 
-def exploit_gather(parts, source, members, kernel_id):
+def exploit_gather(parts, shares, source, members, shards, kernel_id):
     lanes = 128
     total = sum(part.size for part in parts) // lanes
     shape = (members, total // members, lanes)
     vmem = pl.BlockSpec(memory_space=pltpu.VMEM)
     moved = total * lanes * 2
+    fulls = [jax.ShapeDtypeStruct((share.shape[0] * shards, share.shape[1]), share.dtype)
+             for share in shares]
+    sems = [pltpu.SemaphoreType.DMA((len(shares),))] * 6
     return pl.pallas_call(
         functools.partial(gather_kernel, members),
-        out_shape=jax.ShapeDtypeStruct(shape, jnp.bfloat16),
-        in_specs=[pl.BlockSpec(memory_space=pltpu.SMEM)] + [vmem] * len(parts),
-        out_specs=vmem,
+        out_shape=(jax.ShapeDtypeStruct(shape, jnp.bfloat16), *fulls),
+        in_specs=[pl.BlockSpec(memory_space=pltpu.SMEM)] + [vmem] * (len(shares) + len(parts)),
+        out_specs=(vmem,) * 3,
         scratch_shapes=[
             pltpu.VMEM((total, lanes), jnp.bfloat16),
             pltpu.VMEM(shape, jnp.bfloat16),
             pltpu.SemaphoreType.DMA((members,)),
             pltpu.SemaphoreType.DMA((members,)),
-        ],
+        ] + sems,
         compiler_params=pltpu.CompilerParams(
             collective_id=kernel_id, has_side_effects=True, vmem_limit_bytes=48 * 1024 * 1024
         ),
         cost_estimate=pl.CostEstimate(flops=0, transcendentals=0, bytes_accessed=moved * 20),
-    )(source, *parts)
+    )(source, *shares, *parts)
 
 
 def exploit_scatter(packed, kernel_id):
@@ -547,11 +598,10 @@
     own = source[me] == me
 
     up_bf, down_bf = exploit_rows((up_param[0], down_param[0]), source, members, 0)
-    up_full = lax.all_gather(up_bf, "dp", axis=0, tiled=True)
-    down_full = lax.all_gather(down_bf, "dp", axis=0, tiled=True)
     moments = (up_first[0], down_first[0], up_second[0], down_second[0])
-    picked = exploit_gather(moments, source, members, 1)
-    up_full, down_full, picked = lax.optimization_barrier((up_full, down_full, picked))
+    picked, up_full, down_full = exploit_gather(
+        moments, (up_bf, down_bf), source, members, shards, 1
+    )
 
     batch_total = tokens.shape[1] * shards
     up_share, down_share, up_mom, down_mom, up_var_bf, down_var_bf = scatter_with_gradients(

time: 267 us -> 248 us (0.929)
  waiting for transfers between devices: 14.7 us -> 0 us
  between operations: 16.2 us -> 2.8 us
  Pallas kernels: 213 us -> 223 us
    all_gather x2 -> x0, waiting for transfers between devices: 14.6 us -> none  [the longest x1 14.6 us: per_device(): down_full = lax.all_gather(down_bf, 'dp', axis=0, tiled=True)]
    pallas_call x1, Pallas kernels: 78.2 us -> 85.3 us  [scatter_with_gradients(): pl.pallas_call(functools.partial(scatter_compute_kernel, n, batch_total,...]
    pallas_call x1, Pallas kernels: 62.9 us -> 65.9 us  [exploit_gather(): pl.pallas_call(functools.partial(gather_kernel, members), out_shape=(jax....]
  transfers between devices with their start and end apart: 2 -> 0, of which waited for: 1 -> 0; matrix products, arithmetic and copies ran while one was open for 3% -> 0% of each run, Pallas kernels for 24% -> 0%
where the time goes in v4:
time: 248 us; the launch traced here: 247 us
  Pallas kernels  223 us (90%)
  local copies, waits for them, and re-layouts  10.7 us (4%)
  other arithmetic  10.2 us (4%)
  between operations  2.8 us (1%)
    pallas_call x1, Pallas kernels, scatter_with_gradients(): pl.pallas_call(functools.partial(scatter_compute_kernel, n, batch_total,...  85.3 us
    pallas_call x1, Pallas kernels, member_call(): pl.pallas_call(functools.partial(body, n), out_shape=jax.ShapeDtypeStruct...  72.4 us
    pallas_call x1, Pallas kernels, exploit_gather(): pl.pallas_call(functools.partial(gather_kernel, members), out_shape=(jax....  65.9 us
    broadcast_in_dim x2, other arithmetic, per_device(): return tuple((value[None] for value in up_new + down_new))  8.24 us

profile of v4, /device:TPU:1, one launch (start us, length us, event | category | flops | bytes accessed | tf_op | source)
XLA Modules:
  0.0 247.3 jit_solution(12850959852383467277)
XLA Ops:
  0.6 0.0 copy-start.7
  0.6 1.4 convert_element_type.38
  2.1 0.7 convert_element_type.39
  2.8 0.0 copy-done.7
  2.8 0.1 convert_element_type.40
  2.9 0.6 convert_element_type.41
  3.5 0.1 pad.2.clone
  3.5 0.0 copy-start.6
  3.5 0.5 maximum_maximum_fusion.send_ref
  4.0 0.2 copy-done.6
  4.2 72.4 %shard_map.163 = bf16[64,80,128]{2,1,0:T(8,128)(2,1)S(1)} custom-call(s32[64]{0:T(128)S(1)} %copy-done.6, bf16[64,80,128]{2,1,0:T(8,128)(2,1)S(1)} %maximum_maximum_fusion.send_ref), custom_call_target="tpu_custom_call" | custom-call | bytes 26214400 | tf_op jit(solution)/shard_map/pallas_call | solution.py:484
  76.6 1.1 fusion.8
  77.7 0.0 copy-start.2
  77.7 0.0 copy-start.4
  77.7 0.7 reshape.24.up_ref
  78.4 1.7 reshape.25.down_ref
  80.1 0.0 copy-start
  80.1 0.0 copy-done.2
  80.1 0.0 copy-done.4
  80.1 0.0 copy-start.1
  80.1 1.5 copy-done.1
  81.6 0.0 copy-start.5
  81.6 1.1 copy-done.5
  82.6 0.0 copy-start.9
  82.6 65.9 %shard_map.164 = (bf16[64,144,128]{2,1,0:T(8,128)(2,1)}, bf16[768,1536]{1,0:T(8,128)(2,1)}, bf16[1536,768]{1,0:T(8,128)(2,1)}) custom-call(s32[64]{0:T(128)S(1)} %copy-done.6, bf16[192,1536]{1,0:T(8,128)(2,1)S(1)} %reshape.24.up_ref, bf16[384,768]{1,0:T(8,128)(2,1)S(1)} %reshape.25.down_ref, bf16[192,1536]{1,0:T(8,128)(2,1)S(1)} %bitcast.38, ...), custom_call_target="tpu_custom_call" | custom-call | bytes 47185920 | tf_op jit(solution)/shard_map/pallas_call | solution.py:513
  148.5 0.0 copy-done
  148.5 0.0 copy-done.9
  148.5 0.1 copy.20
  148.7 0.0 copy-start.11
  148.7 1.2 reshape_squeeze.3.tokens_ref
  149.9 0.1 copy-done.11
  150.0 1.2 copy.21.classifier_ref
  151.1 85.3 %shard_map.165 = (f32[192,1536]{1,0:T(8,128)}, f32[384,768]{1,0:T(8,128)}, bf16[192,1536]{1,0:T(8,128)(2,1)}, bf16[384,768]{1,0:T(8,128)(2,1)}, bf16[192,1536]{1,0:T(8,128)(2,1)}, /*index=5*/bf16[384,768]{1,0:T(8,128)(2,1)}) custom-call(s32[4]{0:T(128)} %bitcast.40, bf16[64,144,128]{2,1,0:T(8,128)(2,1)} %get-tuple-element.15.send_ref, ...), custom_call_target="tpu_custom_call" | custom-call | flops 11098128384 | bytes 47185920 | tf_op jit(solution)/shard_map/pallas_call | solution.py:448
  236.4 0.6 dynamic_slice.3
  238.9 0.0 copy-start.3
  239.0 0.0 copy-start.8
  239.0 0.0 copy-start.10
  239.0 0.0 copy-start.12
  239.0 0.0 copy-start.13
  239.0 5.5 %fusion.6 = (f32[1,384,768]{2,1,0:T(8,128)}, f32[1,384,768]{2,1,0:T(8,128)}, bf16[1,384,768]{2,1,0:T(8,128)(2,1)}) fusion(f32[384,768]{1,0:T(8,128)} %get-tuple-element.22, bf16[384,768]{1,0:T(8,128)(2,1)} %get-tuple-element.23, pred[]{:T(512)S(6)} %eq.3, f32[1,384,768]{2,1,0:T(8,128)} %param.23, f32[]{:T(128)} %bitcast.35, ...), kind=kLoop, calls=%fused_computation.15 | loop fusion | flops 5898240 | bytes 8257545 | tf_op jit(solution)/shard_map/broadcast_in_dim | solution.py:620
  244.5 0.0 copy-done.3
  244.5 0.0 copy-done.8
  244.5 0.0 copy-done.10
  244.5 0.0 copy-done.12
  244.5 0.0 copy-done.13
  244.5 2.8 %fusion.7 = (f32[1,192,1536]{2,1,0:T(8,128)}, f32[1,192,1536]{2,1,0:T(8,128)}, bf16[1,192,1536]{2,1,0:T(8,128)(2,1)}) fusion(f32[192,1536]{1,0:T(8,128)S(1)} %copy-done.10, bf16[192,1536]{1,0:T(8,128)(2,1)S(1)} %copy-done.13, pred[]{:T(512)S(6)} %eq.3, f32[1,192,1536]{2,1,0:T(8,128)S(1)} %copy-done.3, f32[]{:T(128)} %bitcast.34, ...), kind=kLoop, calls=%fused_computation.16 | loop fusion | flops 5898240 | bytes 8257545 | tf_op jit(solution)/shard_map/broadcast_in_dim | solution.py:620
  (1 shorter events, 0.0 us)
Async XLA Ops:
  0.6 2.2 copy-start.7
  3.5 0.7 copy-start.6
  77.7 2.4 copy-start.2
  77.7 2.4 copy-start.4
  80.1 68.5 %copy-start = (bf16[384,768]{1,0:T(8,128)(2,1)}, bf16[384,768]{1,0:T(8,128)(2,1)S(1)}, u32[]{:S(2)}) copy-start(bf16[384,768]{1,0:T(8,128)(2,1)S(1)} %reshape.25.down_ref) | copy-start | bytes 1769476
  80.1 1.5 copy-start.1
  81.6 1.1 copy-start.5
  82.6 65.9 %copy-start.9 = (bf16[1,4,196,768]{3,1,2,0:T(4,128)(2,1)S(1)}, bf16[1,4,196,768]{3,1,2,0:T(4,128)(2,1)}, u32[]{:S(2)}) copy-start(bf16[1,4,196,768]{3,1,2,0:T(4,128)(2,1)} %param.12) | copy-start | bytes 3612676
  148.7 1.3 copy-start.11
  238.9 5.5 %copy-start.3 = (f32[1,192,1536]{2,1,0:T(8,128)S(1)}, f32[1,192,1536]{2,1,0:T(8,128)}, u32[]{:S(2)}) copy-start(f32[1,192,1536]{2,1,0:T(8,128)} %param.20) | copy-start | bytes 3538948
  239.0 5.5 %copy-start.8 = (f32[1,192,1536]{2,1,0:T(8,128)S(1)}, f32[1,192,1536]{2,1,0:T(8,128)}, u32[]{:S(2)}) copy-start(f32[1,192,1536]{2,1,0:T(8,128)} %param.18) | copy-start | bytes 3538948
  239.0 5.5 %copy-start.10 = (f32[192,1536]{1,0:T(8,128)S(1)}, f32[192,1536]{1,0:T(8,128)}, u32[]{:S(2)}) copy-start(f32[192,1536]{1,0:T(8,128)} %get-tuple-element.19) | copy-start | bytes 3538948
  239.0 5.5 %copy-start.12 = (bf16[192,1536]{1,0:T(8,128)(2,1)S(1)}, bf16[192,1536]{1,0:T(8,128)(2,1)}, u32[]{:S(2)}) copy-start(bf16[192,1536]{1,0:T(8,128)(2,1)} %get-tuple-element.18) | copy-start | bytes 1769476
  239.0 5.5 %copy-start.13 = (bf16[192,1536]{1,0:T(8,128)(2,1)S(1)}, bf16[192,1536]{1,0:T(8,128)(2,1)}, u32[]{:S(2)}) copy-start(bf16[192,1536]{1,0:T(8,128)(2,1)} %get-tuple-element.20) | copy-start | bytes 1769476

commit v5 on v4

--- a/solution.py
+++ b/solution.py
@@ -142,10 +142,12 @@
     transpose(n, me, picked, out_ref, send2, recv2)
 
 
-def gather_kernel(n, source_ref, up_ref, down_ref, *refs):
-    parts = refs[:-13]
-    (out_ref, up_full, down_full, flat, held, send1, recv1,
-     near_send, near_recv, far_send, far_recv, fwd_send, fwd_recv) = refs[-13:]
+def gather_kernel(n, batch_total, patches, source_ref, labels_ref, up_ref, down_ref, tokens_ref,
+                  classifier_ref, *refs):
+    parts = refs[:-17]
+    (out_ref, up_full, down_full, normed_ref, preact_ref, act_ref, delta_ref,
+     flat, held, send1, recv1,
+     near_send, near_recv, far_send, far_recv, fwd_send, fwd_recv) = refs[-17:]
     me = lax.axis_index("member")
     shard = lax.axis_index("dp")
     core = shard % 2
@@ -222,10 +224,18 @@
                for slot, (share, full) in enumerate(shares)]
     for item in forward:
         item.start()
+    for item in near + forward:
+        item.wait()
+    normed, preact, activated, delta = forward_half(
+        tokens_ref[...], labels_ref, up_full[...], down_full[...], classifier_ref[...],
+        batch_total, patches,
+    )
+    normed_ref[...] = normed
+    preact_ref[...] = preact
+    act_ref[...] = activated
+    delta_ref[...] = delta
     lax.fori_loop(1, n, finish, 0)
     pick_rows(n, source_ref, held, out_ref)
-    for item in near + forward:
-        item.wait()
 
 
 def scatter_kernel(n, send_ref, out_ref, send1, recv1):
@@ -234,7 +244,7 @@
     transpose(n, me, send_ref, out_ref, send1, recv1)
 
 
-def block_gradients(tokens, labels_ref, up_weight, down_weight, classifier, batch_total, patches):
+def forward_half(tokens, labels_ref, up_weight, down_weight, classifier, batch_total, patches):
     tokens_n, features = tokens.shape
     hidden_units = up_weight.shape[1]
     classes = classifier.shape[1]
@@ -286,6 +296,12 @@
         - out_normed * jnp.mean(token_delta * out_normed, axis=1, keepdims=True)
     )
     residual_delta = residual_delta.astype(jnp.bfloat16)
+    return normed, preact, activated, residual_delta
+
+
+def backward_half(normed, preact, activated, residual_delta, down_weight):
+    features = normed.shape[1]
+    hidden_units = preact.shape[1]
     down_scale = hidden_units ** (-0.5)
     down_gradient = (
         lax.dot_general(
@@ -311,7 +327,7 @@
 
 
 def scatter_compute_kernel(
-    n, batch_total, patches, labels_ref, send_ref, tokens_ref, up_ref, down_ref, classifier_ref,
+    n, send_ref, normed_ref, preact_ref, act_ref, delta_ref, down_ref,
     up_share_ref, down_share_ref, up_first_ref, down_first_ref, up_second_ref, down_second_ref,
     flat, up_term, down_term, up_near, down_near, up_part, down_part, up_far, down_far,
     send_sem, recv_sem, near_send, near_recv, far_send, far_recv,
@@ -360,9 +376,8 @@
 
     lax.fori_loop(1, n, start, 0)
     flat[pl.ds(pl.multiple_of(me * chunk, 16), chunk)] = send_ref[me]
-    up_gradient, down_gradient = block_gradients(
-        tokens_ref[...], labels_ref, up_ref[...], down_ref[...], classifier_ref[...],
-        batch_total, patches,
+    up_gradient, down_gradient = backward_half(
+        normed_ref[...], preact_ref[...], act_ref[...], delta_ref[...], down_ref[...]
     )
     up_term[...] = up_gradient.astype(jnp.bfloat16)
     down_term[...] = down_gradient.astype(jnp.bfloat16)
@@ -435,23 +450,23 @@
             offset += rows
 
 
-def scatter_with_gradients(picked, tokens, labels, up_full, down_full, classifier, batch_total,
+def scatter_with_gradients(picked, normed, preact, activated, delta, up_full, down_full,
                            kernel_id):
     n = picked.shape[0]
-    images, patches, features = tokens.shape
+    tokens_n, features = normed.shape
     vmem = pl.BlockSpec(memory_space=pltpu.VMEM)
     moved = picked.size * picked.dtype.itemsize
-    flops = 12 * images * patches * features * up_full.shape[1]
+    flops = 6 * tokens_n * features * up_full.shape[1]
     up_rows = (up_full.shape[0] // 4, up_full.shape[1])
     down_rows = (down_full.shape[0] // 4, down_full.shape[1])
     bf16 = jnp.bfloat16
     return pl.pallas_call(
-        functools.partial(scatter_compute_kernel, n, batch_total, patches),
+        functools.partial(scatter_compute_kernel, n),
         out_shape=(
             jax.ShapeDtypeStruct(up_rows, jnp.float32),
             jax.ShapeDtypeStruct(down_rows, jnp.float32),
         ) + tuple(jax.ShapeDtypeStruct(shape, bf16) for shape in (up_rows, down_rows) * 2),
-        in_specs=[pl.BlockSpec(memory_space=pltpu.SMEM)] + [vmem] * 5,
+        in_specs=[vmem] * 6,
         out_specs=(vmem,) * 6,
         scratch_shapes=[
             pltpu.VMEM((picked.shape[0] * picked.shape[1], picked.shape[2]), bf16),
@@ -474,7 +489,7 @@
             collective_id=kernel_id, has_side_effects=True, vmem_limit_bytes=63 * 1024 * 1024
         ),
         cost_estimate=pl.CostEstimate(flops=flops, transcendentals=0, bytes_accessed=moved * 20),
-    )(labels, picked, tokens.reshape(images * patches, features), up_full, down_full, classifier)
+    )(picked, normed, preact, activated, delta, down_full)
 
 
 def member_call(body, packed, operands, scratch, kernel_id):
@@ -501,7 +516,11 @@
     return member_call(exploit_kernel, packed, (source, packed), [block, block] + sems, kernel_id)
 
 
-def exploit_gather(parts, shares, source, members, shards, kernel_id):
+def exploit_gather(parts, shares, source, tokens, labels, classifier, batch_total, members,
+                   shards, kernel_id):
+    images, patches, features = tokens.shape
+    tokens_n = images * patches
+    hidden = shares[0].shape[1]
     lanes = 128
     total = sum(part.size for part in parts) // lanes
     shape = (members, total // members, lanes)
@@ -511,10 +530,18 @@
              for share in shares]
     sems = [pltpu.SemaphoreType.DMA((len(shares),))] * 6
     return pl.pallas_call(
-        functools.partial(gather_kernel, members),
-        out_shape=(jax.ShapeDtypeStruct(shape, jnp.bfloat16), *fulls),
-        in_specs=[pl.BlockSpec(memory_space=pltpu.SMEM)] + [vmem] * (len(shares) + len(parts)),
-        out_specs=(vmem,) * 3,
+        functools.partial(gather_kernel, members, batch_total, patches),
+        out_shape=(
+            jax.ShapeDtypeStruct(shape, jnp.bfloat16),
+            *fulls,
+            jax.ShapeDtypeStruct((tokens_n, features), jnp.bfloat16),
+            jax.ShapeDtypeStruct((tokens_n, hidden), jnp.float32),
+            jax.ShapeDtypeStruct((tokens_n, hidden), jnp.bfloat16),
+            jax.ShapeDtypeStruct((tokens_n, features), jnp.bfloat16),
+        ),
+        in_specs=[pl.BlockSpec(memory_space=pltpu.SMEM)] * 2
+        + [vmem] * (len(shares) + 2 + len(parts)),
+        out_specs=(vmem,) * 7,
         scratch_shapes=[
             pltpu.VMEM((total, lanes), jnp.bfloat16),
             pltpu.VMEM(shape, jnp.bfloat16),
@@ -522,10 +549,10 @@
             pltpu.SemaphoreType.DMA((members,)),
         ] + sems,
         compiler_params=pltpu.CompilerParams(
-            collective_id=kernel_id, has_side_effects=True, vmem_limit_bytes=48 * 1024 * 1024
+            collective_id=kernel_id, has_side_effects=True, vmem_limit_bytes=63 * 1024 * 1024
         ),
         cost_estimate=pl.CostEstimate(flops=0, transcendentals=0, bytes_accessed=moved * 20),
-    )(source, *shares, *parts)
+    )(source, labels, *shares, tokens.reshape(tokens_n, features), classifier, *parts)
 
 
 def exploit_scatter(packed, kernel_id):
@@ -599,13 +626,13 @@
 
     up_bf, down_bf = exploit_rows((up_param[0], down_param[0]), source, members, 0)
     moments = (up_first[0], down_first[0], up_second[0], down_second[0])
-    picked, up_full, down_full = exploit_gather(
-        moments, (up_bf, down_bf), source, members, shards, 1
-    )
-
     batch_total = tokens.shape[1] * shards
+    picked, up_full, down_full, normed, preact, activated, delta = exploit_gather(
+        moments, (up_bf, down_bf), source, tokens[0], labels[0], classifier, batch_total,
+        members, shards, 1,
+    )
     up_share, down_share, up_mom, down_mom, up_var_bf, down_var_bf = scatter_with_gradients(
-        picked, tokens[0], labels[0], up_full, down_full, classifier, batch_total, 2
+        picked, normed, preact, activated, delta, up_full, down_full, 2
     )
 
     up_now = jnp.where(own, up_param[0], up_bf.astype(jnp.float32))

time: 248 us -> 247 us (level)
  Pallas kernels: 223 us -> 226 us
  local copies, waits for them, and re-layouts: 10.7 us -> 7.87 us
    unnamed x30 -> x26, local copies, waits for them, and re-layouts: 4.1 us -> 1.6 us
where the time goes in v5:
time: 247 us; the launch traced here: 246 us
  Pallas kernels  226 us (91%)
  other arithmetic  10.1 us (4%)
  local copies, waits for them, and re-layouts  7.87 us (3%)
  between operations  2.8 us (1%)
    pallas_call x1, Pallas kernels, scatter_with_gradients(): pl.pallas_call(functools.partial(scatter_compute_kernel, n), out_shape=(j...  77.9 us
    pallas_call x1, Pallas kernels, exploit_gather(): pl.pallas_call(functools.partial(gather_kernel, members, batch_total, pat...  75.5 us
    pallas_call x1, Pallas kernels, member_call(): pl.pallas_call(functools.partial(body, n), out_shape=jax.ShapeDtypeStruct...  72.4 us
    broadcast_in_dim x2, other arithmetic, per_device(): return tuple((value[None] for value in up_new + down_new))  8.07 us

profile of v5, /device:TPU:1, one launch (start us, length us, event | category | flops | bytes accessed | tf_op | source)
XLA Modules:
  0.0 246.4 jit_solution(5041372657103818211)
XLA Ops:
  0.6 0.0 copy-start.4
  0.6 1.4 convert_element_type.38
  2.1 0.7 convert_element_type.39
  2.8 0.0 copy-done.4
  2.8 0.1 convert_element_type.40
  2.9 0.6 convert_element_type.41
  3.5 0.1 pad.2.clone
  3.5 0.0 copy-start
  3.5 0.5 maximum_maximum_fusion.send_ref
  4.0 0.2 copy-done
  4.2 72.4 %shard_map.163 = bf16[64,80,128]{2,1,0:T(8,128)(2,1)S(1)} custom-call(s32[64]{0:T(128)S(1)} %copy-done, bf16[64,80,128]{2,1,0:T(8,128)(2,1)S(1)} %maximum_maximum_fusion.send_ref), custom_call_target="tpu_custom_call" | custom-call | bytes 26214400 | tf_op jit(solution)/shard_map/pallas_call | solution.py:499
  76.6 0.3 fusion.8
  76.8 0.0 copy-start.7
  76.9 1.5 reshape.24.up_ref
  78.3 1.4 reshape.25.down_ref
  79.7 0.0 copy-done.7
  79.7 0.1 copy.20
  79.9 0.0 copy-start.9
  79.9 1.2 reshape_squeeze.3.tokens_ref
  81.0 0.1 copy-done.9
  81.2 1.2 copy.21.classifier_ref
  82.3 75.5 %shard_map.164 = (bf16[64,144,128]{2,1,0:T(8,128)(2,1)}, bf16[768,1536]{1,0:T(8,128)(2,1)}, bf16[1536,768]{1,0:T(8,128)(2,1)}, bf16[784,768]{1,0:T(8,128)(2,1)},...) custom-call(s32[64]{0:T(128)} %source_ref.3, s32[4]{0:T(128)} %bitcast.40, ...), custom_call_target="tpu_custom_call" | custom-call | bytes 47185920 | tf_op jit(solution)/shard_map/pallas_call | solution.py:532
  157.8 0.0 copy-start.1
  157.8 0.0 copy-start.3
  157.8 77.9 %shard_map.165 = (f32[192,1536]{1,0:T(8,128)}, f32[384,768]{1,0:T(8,128)}, bf16[192,1536]{1,0:T(8,128)(2,1)}, bf16[384,768]{1,0:T(8,128)(2,1)}, bf16[192,1536]{1,0:T(8,128)(2,1)}, /*index=5*/bf16[384,768]{1,0:T(8,128)(2,1)}) custom-call(bf16[64,144,128]{2,1,0:T(8,128)(2,1)} %get-tuple-element.18.send_ref, bf16[784,768]{1,0:T(8,128)(2,1)} %get-tuple-element.19.normed_ref, ...), custom_call_target="tpu_custom_call" | custom-call | flops 5549064192 | bytes 47185920 | tf_op jit(solution)/shard_map/pallas_call | solution.py:463
  235.7 0.0 copy-done.1
  235.7 0.6 dynamic_slice.3
  238.3 0.0 copy-done.3
  238.3 0.0 copy-start.2
  238.3 0.0 copy-start.5
  238.3 0.0 copy-start.6
  238.3 0.0 copy-start.8
  238.3 0.0 copy-start.10
  238.3 0.0 copy-start.11
  238.3 5.3 %fusion.6 = (f32[1,384,768]{2,1,0:T(8,128)}, f32[1,384,768]{2,1,0:T(8,128)}, bf16[1,384,768]{2,1,0:T(8,128)(2,1)}) fusion(f32[384,768]{1,0:T(8,128)} %get-tuple-element.28, bf16[384,768]{1,0:T(8,128)(2,1)} %get-tuple-element.29, pred[]{:T(512)S(6)} %eq.3, f32[1,384,768]{2,1,0:T(8,128)} %param.23, f32[]{:T(128)} %bitcast.35, ...), kind=kLoop, calls=%fused_computation.15 | loop fusion | flops 5898240 | bytes 8257545 | tf_op jit(solution)/shard_map/broadcast_in_dim | solution.py:647
  243.6 0.0 copy-done.2
  243.6 0.0 copy-done.5
  243.6 0.0 copy-done.6
  243.6 0.0 copy-done.8
  243.7 0.0 copy-done.10
  243.7 0.0 copy-done.11
  243.7 2.8 %fusion.7 = (f32[1,192,1536]{2,1,0:T(8,128)}, f32[1,192,1536]{2,1,0:T(8,128)}, bf16[1,192,1536]{2,1,0:T(8,128)(2,1)}) fusion(f32[192,1536]{1,0:T(8,128)S(1)} %copy-done.8, bf16[192,1536]{1,0:T(8,128)(2,1)S(1)} %copy-done.11, pred[]{:T(512)S(6)} %eq.3, f32[1,192,1536]{2,1,0:T(8,128)S(1)} %copy-done.6, f32[]{:T(128)} %bitcast.34, ...), kind=kLoop, calls=%fused_computation.16 | loop fusion | flops 5898240 | bytes 8257545 | tf_op jit(solution)/shard_map/broadcast_in_dim | solution.py:647
  (1 shorter events, 0.0 us)
Async XLA Ops:
  0.6 2.2 copy-start.4
  3.5 0.7 copy-start
  76.8 2.9 %copy-start.7 = (bf16[1,4,196,768]{3,1,2,0:T(4,128)(2,1)S(1)}, bf16[1,4,196,768]{3,1,2,0:T(4,128)(2,1)}, u32[]{:S(2)}) copy-start(bf16[1,4,196,768]{3,1,2,0:T(4,128)(2,1)} %param.12) | copy-start | bytes 3612676
  79.9 1.3 copy-start.9
  157.8 78.0 %copy-start.1 = (s32[64]{0:T(128)S(1)}, s32[64]{0:T(128)}, u32[]{:S(2)}) copy-start(s32[64]{0:T(128)} %source_ref.3) | copy-start | bytes 772
  157.8 80.5 %copy-start.3 = (bf16[384,768]{1,0:T(8,128)(2,1)S(1)}, bf16[384,768]{1,0:T(8,128)(2,1)}, u32[]{:S(2)}) copy-start(bf16[384,768]{1,0:T(8,128)(2,1)} %reshape.25.down_ref) | copy-start | bytes 1769476
  238.3 5.4 %copy-start.2 = (bf16[192,1536]{1,0:T(8,128)(2,1)S(1)}, bf16[192,1536]{1,0:T(8,128)(2,1)}, u32[]{:S(2)}) copy-start(bf16[192,1536]{1,0:T(8,128)(2,1)} %reshape.24.up_ref) | copy-start | bytes 1769476
  238.3 5.4 %copy-start.5 = (f32[1,192,1536]{2,1,0:T(8,128)S(1)}, f32[1,192,1536]{2,1,0:T(8,128)}, u32[]{:S(2)}) copy-start(f32[1,192,1536]{2,1,0:T(8,128)} %param.18) | copy-start | bytes 3538948
  238.3 5.3 %copy-start.6 = (f32[1,192,1536]{2,1,0:T(8,128)S(1)}, f32[1,192,1536]{2,1,0:T(8,128)}, u32[]{:S(2)}) copy-start(f32[1,192,1536]{2,1,0:T(8,128)} %param.20) | copy-start | bytes 3538948
  238.3 5.3 %copy-start.8 = (f32[192,1536]{1,0:T(8,128)S(1)}, f32[192,1536]{1,0:T(8,128)}, u32[]{:S(2)}) copy-start(f32[192,1536]{1,0:T(8,128)} %get-tuple-element.25) | copy-start | bytes 3538948
  238.3 5.3 %copy-start.10 = (bf16[192,1536]{1,0:T(8,128)(2,1)S(1)}, bf16[192,1536]{1,0:T(8,128)(2,1)}, u32[]{:S(2)}) copy-start(bf16[192,1536]{1,0:T(8,128)(2,1)} %get-tuple-element.24) | copy-start | bytes 1769476
  238.3 5.3 %copy-start.11 = (bf16[192,1536]{1,0:T(8,128)(2,1)S(1)}, bf16[192,1536]{1,0:T(8,128)(2,1)}, u32[]{:S(2)}) copy-start(bf16[192,1536]{1,0:T(8,128)(2,1)} %get-tuple-element.26) | copy-start | bytes 1769476

commit v6 on v5

--- a/solution.py
+++ b/solution.py
@@ -374,7 +374,7 @@
         copy(k).wait()
         return carry
 
-    lax.fori_loop(1, n, start, 0)
+    lax.fori_loop(1, n // 2, start, 0)
     flat[pl.ds(pl.multiple_of(me * chunk, 16), chunk)] = send_ref[me]
     up_gradient, down_gradient = backward_half(
         normed_ref[...], preact_ref[...], act_ref[...], delta_ref[...], down_ref[...]
@@ -428,6 +428,7 @@
         slot += 1
     for item in far:
         item.start()
+    lax.fori_loop(n // 2, n, start, 0)
     for item in far:
         item.wait()
 

time: 247 us -> 251 us (1.016)
  Pallas kernels: 226 us -> 230 us
    pallas_call x1, Pallas kernels: 77.9 us -> 82.6 us  [scatter_with_gradients(): pl.pallas_call(functools.partial(scatter_compute_kernel, n), out_shape=(j...]
where the time goes in v6:
time: 251 us
  Pallas kernels  230 us (92%)
  other arithmetic  10.1 us (4%)
  local copies, waits for them, and re-layouts  7.87 us (3%)
  between operations  2.8 us (1%)
    pallas_call x1, Pallas kernels, scatter_with_gradients(): pl.pallas_call(functools.partial(scatter_compute_kernel, n), out_shape=(j...  82.6 us
    pallas_call x1, Pallas kernels, exploit_gather(): pl.pallas_call(functools.partial(gather_kernel, members, batch_total, pat...  75.5 us
    pallas_call x1, Pallas kernels, member_call(): pl.pallas_call(functools.partial(body, n), out_shape=jax.ShapeDtypeStruct...  72.4 us
    broadcast_in_dim x2, other arithmetic, per_device(): return tuple((value[None] for value in up_new + down_new))  8.07 us

profile of v6, /device:TPU:1, one launch (start us, length us, event | category | flops | bytes accessed | tf_op | source)
XLA Modules:
  0.0 251.1 jit_solution(17977447029254682532)
XLA Ops:
  0.6 0.0 copy-start.4
  0.6 1.4 convert_element_type.38
  2.1 0.7 convert_element_type.39
  2.8 0.0 copy-done.4
  2.8 0.1 convert_element_type.40
  2.9 0.6 convert_element_type.41
  3.5 0.1 pad.2.clone
  3.5 0.0 copy-start
  3.5 0.5 maximum_maximum_fusion.send_ref
  4.0 0.2 copy-done
  4.2 72.4 %shard_map.163 = bf16[64,80,128]{2,1,0:T(8,128)(2,1)S(1)} custom-call(s32[64]{0:T(128)S(1)} %copy-done, bf16[64,80,128]{2,1,0:T(8,128)(2,1)S(1)} %maximum_maximum_fusion.send_ref), custom_call_target="tpu_custom_call" | custom-call | bytes 26214400 | tf_op jit(solution)/shard_map/pallas_call | solution.py:500
  76.6 0.3 fusion.8
  76.8 0.0 copy-start.7
  76.9 1.5 reshape.24.up_ref
  78.3 1.4 reshape.25.down_ref
  79.7 0.0 copy-done.7
  79.7 0.1 copy.20
  79.9 0.0 copy-start.9
  79.9 1.2 reshape_squeeze.3.tokens_ref
  81.0 0.1 copy-done.9
  81.2 1.2 copy.21.classifier_ref
  82.3 75.5 %shard_map.164 = (bf16[64,144,128]{2,1,0:T(8,128)(2,1)}, bf16[768,1536]{1,0:T(8,128)(2,1)}, bf16[1536,768]{1,0:T(8,128)(2,1)}, bf16[784,768]{1,0:T(8,128)(2,1)},...) custom-call(s32[64]{0:T(128)} %source_ref.3, s32[4]{0:T(128)} %bitcast.40, ...), custom_call_target="tpu_custom_call" | custom-call | bytes 47185920 | tf_op jit(solution)/shard_map/pallas_call | solution.py:533
  157.8 0.0 copy-start.1
  157.8 0.0 copy-start.3
  157.8 82.6 %shard_map.165 = (f32[192,1536]{1,0:T(8,128)}, f32[384,768]{1,0:T(8,128)}, bf16[192,1536]{1,0:T(8,128)(2,1)}, bf16[384,768]{1,0:T(8,128)(2,1)}, bf16[192,1536]{1,0:T(8,128)(2,1)}, /*index=5*/bf16[384,768]{1,0:T(8,128)(2,1)}) custom-call(bf16[64,144,128]{2,1,0:T(8,128)(2,1)} %get-tuple-element.18.send_ref, bf16[784,768]{1,0:T(8,128)(2,1)} %get-tuple-element.19.normed_ref, ...), custom_call_target="tpu_custom_call" | custom-call | flops 5549064192 | bytes 47185920 | tf_op jit(solution)/shard_map/pallas_call | solution.py:464
  240.4 0.0 copy-done.1
  240.4 0.6 dynamic_slice.3
  242.9 0.0 copy-done.3
  242.9 0.0 copy-start.2
  243.0 0.0 copy-start.5
  243.0 0.0 copy-start.6
  243.0 0.0 copy-start.8
  243.0 0.0 copy-start.10
  243.0 0.0 copy-start.11
  243.0 5.3 %fusion.6 = (f32[1,384,768]{2,1,0:T(8,128)}, f32[1,384,768]{2,1,0:T(8,128)}, bf16[1,384,768]{2,1,0:T(8,128)(2,1)}) fusion(f32[384,768]{1,0:T(8,128)} %get-tuple-element.28, bf16[384,768]{1,0:T(8,128)(2,1)} %get-tuple-element.29, pred[]{:T(512)S(6)} %eq.3, f32[1,384,768]{2,1,0:T(8,128)} %param.23, f32[]{:T(128)} %bitcast.35, ...), kind=kLoop, calls=%fused_computation.15 | loop fusion | flops 5898240 | bytes 8257545 | tf_op jit(solution)/shard_map/broadcast_in_dim | solution.py:648
  248.3 0.0 copy-done.2
  248.3 0.0 copy-done.5
  248.3 0.0 copy-done.6
  248.3 0.0 copy-done.8
  248.3 0.0 copy-done.10
  248.3 0.0 copy-done.11
  248.3 2.8 %fusion.7 = (f32[1,192,1536]{2,1,0:T(8,128)}, f32[1,192,1536]{2,1,0:T(8,128)}, bf16[1,192,1536]{2,1,0:T(8,128)(2,1)}) fusion(f32[192,1536]{1,0:T(8,128)S(1)} %copy-done.8, bf16[192,1536]{1,0:T(8,128)(2,1)S(1)} %copy-done.11, pred[]{:T(512)S(6)} %eq.3, f32[1,192,1536]{2,1,0:T(8,128)S(1)} %copy-done.6, f32[]{:T(128)} %bitcast.34, ...), kind=kLoop, calls=%fused_computation.16 | loop fusion | flops 5898240 | bytes 8257545 | tf_op jit(solution)/shard_map/broadcast_in_dim | solution.py:648
  (1 shorter events, 0.0 us)
Async XLA Ops:
  0.6 2.2 copy-start.4
  3.5 0.7 copy-start
  76.8 2.9 %copy-start.7 = (bf16[1,4,196,768]{3,1,2,0:T(4,128)(2,1)S(1)}, bf16[1,4,196,768]{3,1,2,0:T(4,128)(2,1)}, u32[]{:S(2)}) copy-start(bf16[1,4,196,768]{3,1,2,0:T(4,128)(2,1)} %param.12) | copy-start | bytes 3612676
  79.9 1.3 copy-start.9
  157.8 82.6 %copy-start.1 = (s32[64]{0:T(128)S(1)}, s32[64]{0:T(128)}, u32[]{:S(2)}) copy-start(s32[64]{0:T(128)} %source_ref.3) | copy-start | bytes 772
  157.8 85.2 %copy-start.3 = (bf16[384,768]{1,0:T(8,128)(2,1)S(1)}, bf16[384,768]{1,0:T(8,128)(2,1)}, u32[]{:S(2)}) copy-start(bf16[384,768]{1,0:T(8,128)(2,1)} %reshape.25.down_ref) | copy-start | bytes 1769476
  242.9 5.4 %copy-start.2 = (bf16[192,1536]{1,0:T(8,128)(2,1)S(1)}, bf16[192,1536]{1,0:T(8,128)(2,1)}, u32[]{:S(2)}) copy-start(bf16[192,1536]{1,0:T(8,128)(2,1)} %reshape.24.up_ref) | copy-start | bytes 1769476
  243.0 5.4 %copy-start.5 = (f32[1,192,1536]{2,1,0:T(8,128)S(1)}, f32[1,192,1536]{2,1,0:T(8,128)}, u32[]{:S(2)}) copy-start(f32[1,192,1536]{2,1,0:T(8,128)} %param.18) | copy-start | bytes 3538948
  243.0 5.3 %copy-start.6 = (f32[1,192,1536]{2,1,0:T(8,128)S(1)}, f32[1,192,1536]{2,1,0:T(8,128)}, u32[]{:S(2)}) copy-start(f32[1,192,1536]{2,1,0:T(8,128)} %param.20) | copy-start | bytes 3538948
  243.0 5.3 %copy-start.8 = (f32[192,1536]{1,0:T(8,128)S(1)}, f32[192,1536]{1,0:T(8,128)}, u32[]{:S(2)}) copy-start(f32[192,1536]{1,0:T(8,128)} %get-tuple-element.25) | copy-start | bytes 3538948
  243.0 5.3 %copy-start.10 = (bf16[192,1536]{1,0:T(8,128)(2,1)S(1)}, bf16[192,1536]{1,0:T(8,128)(2,1)}, u32[]{:S(2)}) copy-start(bf16[192,1536]{1,0:T(8,128)(2,1)} %get-tuple-element.24) | copy-start | bytes 1769476
  243.0 5.3 %copy-start.11 = (bf16[192,1536]{1,0:T(8,128)(2,1)S(1)}, bf16[192,1536]{1,0:T(8,128)(2,1)}, u32[]{:S(2)}) copy-start(bf16[192,1536]{1,0:T(8,128)(2,1)} %get-tuple-element.26) | copy-start | bytes 1769476

commit v7 on v5

--- a/solution.py
+++ b/solution.py
@@ -574,7 +574,7 @@
 def exploit_rows(parts, source, members, kernel_id):
     lanes = 128
     rows = [part.size // (members * lanes) for part in parts]
-    pad = -sum(rows) % 16
+    pad = 0
     pieces = [part.astype(jnp.bfloat16).reshape(members, -1, lanes) for part in parts]
     if pad:
         pieces.append(jnp.zeros((members, pad, lanes), jnp.bfloat16))

time: 247 us -> 245 us (level)
    pallas_call x1, Pallas kernels: 72.4 us -> 67 us  [member_call(): pl.pallas_call(functools.partial(body, n), out_shape=jax.ShapeDtypeStruct...]
    pallas_call x1, Pallas kernels: 77.9 us -> 82 us  [scatter_with_gradients(): pl.pallas_call(functools.partial(scatter_compute_kernel, n), out_shape=(j...]
where the time goes in v7:
time: 245 us; the launch traced here: 244 us
  Pallas kernels  224 us (91%)
  other arithmetic  9.86 us (4%)
  local copies, waits for them, and re-layouts  7.97 us (3%)
  between operations  2.8 us (1%)
    pallas_call x1, Pallas kernels, scatter_with_gradients(): pl.pallas_call(functools.partial(scatter_compute_kernel, n), out_shape=(j...  82 us
    pallas_call x1, Pallas kernels, exploit_gather(): pl.pallas_call(functools.partial(gather_kernel, members, batch_total, pat...  74.8 us
    pallas_call x1, Pallas kernels, member_call(): pl.pallas_call(functools.partial(body, n), out_shape=jax.ShapeDtypeStruct...  67 us
    broadcast_in_dim x2, other arithmetic, per_device(): return tuple((value[None] for value in up_new + down_new))  8.07 us

profile of v7, /device:TPU:1, one launch (start us, length us, event | category | flops | bytes accessed | tf_op | source)
XLA Modules:
  0.0 244.4 jit_solution(14233780805937502223)
XLA Ops:
  0.6 0.0 copy-start.4
  0.6 1.4 convert_element_type.38
  2.1 0.7 convert_element_type.39
  2.8 0.0 copy-done.4
  2.8 0.1 convert_element_type.40
  2.9 0.6 convert_element_type.41
  3.4 0.0 copy-start
  3.5 0.3 pad_maximum_fusion.send_ref
  3.8 0.3 copy-done
  4.1 67.0 %shard_map.163 = bf16[64,72,128]{2,1,0:T(8,128)(2,1)S(1)} custom-call(s32[64]{0:T(128)S(1)} %copy-done, bf16[64,72,128]{2,1,0:T(8,128)(2,1)S(1)} %pad_maximum_fusion.send_ref), custom_call_target="tpu_custom_call" | custom-call | bytes 23592960 | tf_op jit(solution)/shard_map/pallas_call | solution.py:499
  71.1 0.3 fusion.8
  71.4 0.0 copy-start.7
  71.4 1.5 reshape.24.up_ref
  72.9 1.4 reshape.25.down_ref
  74.3 0.0 copy-done.7
  74.3 0.1 copy.20
  74.4 0.0 copy-start.9
  74.4 1.2 reshape_squeeze.3.tokens_ref
  75.6 0.1 copy-done.9
  75.7 1.2 copy.21.classifier_ref
  76.9 74.8 %shard_map.164 = (bf16[64,144,128]{2,1,0:T(8,128)(2,1)}, bf16[768,1536]{1,0:T(8,128)(2,1)}, bf16[1536,768]{1,0:T(8,128)(2,1)}, bf16[784,768]{1,0:T(8,128)(2,1)},...) custom-call(s32[64]{0:T(128)} %source_ref.3, s32[4]{0:T(128)} %bitcast.40, ...), custom_call_target="tpu_custom_call" | custom-call | bytes 47185920 | tf_op jit(solution)/shard_map/pallas_call | solution.py:532
  151.6 0.0 copy-start.1
  151.6 0.0 copy-start.3
  151.7 82.0 %shard_map.165 = (f32[192,1536]{1,0:T(8,128)}, f32[384,768]{1,0:T(8,128)}, bf16[192,1536]{1,0:T(8,128)(2,1)}, bf16[384,768]{1,0:T(8,128)(2,1)}, bf16[192,1536]{1,0:T(8,128)(2,1)}, /*index=5*/bf16[384,768]{1,0:T(8,128)(2,1)}) custom-call(bf16[64,144,128]{2,1,0:T(8,128)(2,1)} %get-tuple-element.18.send_ref, bf16[784,768]{1,0:T(8,128)(2,1)} %get-tuple-element.19.normed_ref, ...), custom_call_target="tpu_custom_call" | custom-call | flops 5549064192 | bytes 47185920 | tf_op jit(solution)/shard_map/pallas_call | solution.py:463
  233.7 0.0 copy-done.1
  233.7 0.6 dynamic_slice.3
  236.2 0.0 copy-done.3
  236.2 0.0 copy-start.2
  236.2 0.0 copy-start.5
  236.2 0.0 copy-start.6
  236.3 0.0 copy-start.8
  236.3 0.0 copy-start.10
  236.3 0.0 copy-start.11
  236.3 5.3 %fusion.6 = (f32[1,384,768]{2,1,0:T(8,128)}, f32[1,384,768]{2,1,0:T(8,128)}, bf16[1,384,768]{2,1,0:T(8,128)(2,1)}) fusion(f32[384,768]{1,0:T(8,128)} %get-tuple-element.28, bf16[384,768]{1,0:T(8,128)(2,1)} %get-tuple-element.29, pred[]{:T(512)S(6)} %eq.3, f32[1,384,768]{2,1,0:T(8,128)} %param.23, f32[]{:T(128)} %bitcast.35, ...), kind=kLoop, calls=%fused_computation.15 | loop fusion | flops 5898240 | bytes 8257545 | tf_op jit(solution)/shard_map/broadcast_in_dim | solution.py:647
  241.6 0.0 copy-done.2
  241.6 0.0 copy-done.5
  241.6 0.0 copy-done.6
  241.6 0.0 copy-done.8
  241.6 0.0 copy-done.10
  241.6 0.0 copy-done.11
  241.6 2.8 %fusion.7 = (f32[1,192,1536]{2,1,0:T(8,128)}, f32[1,192,1536]{2,1,0:T(8,128)}, bf16[1,192,1536]{2,1,0:T(8,128)(2,1)}) fusion(f32[192,1536]{1,0:T(8,128)S(1)} %copy-done.8, bf16[192,1536]{1,0:T(8,128)(2,1)S(1)} %copy-done.11, pred[]{:T(512)S(6)} %eq.3, f32[1,192,1536]{2,1,0:T(8,128)S(1)} %copy-done.6, f32[]{:T(128)} %bitcast.34, ...), kind=kLoop, calls=%fused_computation.16 | loop fusion | flops 5898240 | bytes 8257545 | tf_op jit(solution)/shard_map/broadcast_in_dim | solution.py:647
Async XLA Ops:
  0.6 2.2 copy-start.4
  3.4 0.7 copy-start
  71.4 2.9 %copy-start.7 = (bf16[1,4,196,768]{3,1,2,0:T(4,128)(2,1)S(1)}, bf16[1,4,196,768]{3,1,2,0:T(4,128)(2,1)}, u32[]{:S(2)}) copy-start(bf16[1,4,196,768]{3,1,2,0:T(4,128)(2,1)} %param.12) | copy-start | bytes 3612676
  74.4 1.3 copy-start.9
  151.6 82.0 %copy-start.1 = (s32[64]{0:T(128)S(1)}, s32[64]{0:T(128)}, u32[]{:S(2)}) copy-start(s32[64]{0:T(128)} %source_ref.3) | copy-start | bytes 772
  151.6 84.6 %copy-start.3 = (bf16[384,768]{1,0:T(8,128)(2,1)S(1)}, bf16[384,768]{1,0:T(8,128)(2,1)}, u32[]{:S(2)}) copy-start(bf16[384,768]{1,0:T(8,128)(2,1)} %reshape.25.down_ref) | copy-start | bytes 1769476
  236.2 5.4 %copy-start.2 = (bf16[192,1536]{1,0:T(8,128)(2,1)S(1)}, bf16[192,1536]{1,0:T(8,128)(2,1)}, u32[]{:S(2)}) copy-start(bf16[192,1536]{1,0:T(8,128)(2,1)} %reshape.24.up_ref) | copy-start | bytes 1769476
  236.2 5.4 %copy-start.5 = (f32[1,192,1536]{2,1,0:T(8,128)S(1)}, f32[1,192,1536]{2,1,0:T(8,128)}, u32[]{:S(2)}) copy-start(f32[1,192,1536]{2,1,0:T(8,128)} %param.18) | copy-start | bytes 3538948
  236.2 5.3 %copy-start.6 = (f32[1,192,1536]{2,1,0:T(8,128)S(1)}, f32[1,192,1536]{2,1,0:T(8,128)}, u32[]{:S(2)}) copy-start(f32[1,192,1536]{2,1,0:T(8,128)} %param.20) | copy-start | bytes 3538948
  236.3 5.3 %copy-start.8 = (f32[192,1536]{1,0:T(8,128)S(1)}, f32[192,1536]{1,0:T(8,128)}, u32[]{:S(2)}) copy-start(f32[192,1536]{1,0:T(8,128)} %get-tuple-element.25) | copy-start | bytes 3538948
  236.3 5.3 %copy-start.10 = (bf16[192,1536]{1,0:T(8,128)(2,1)S(1)}, bf16[192,1536]{1,0:T(8,128)(2,1)}, u32[]{:S(2)}) copy-start(bf16[192,1536]{1,0:T(8,128)(2,1)} %get-tuple-element.24) | copy-start | bytes 1769476
  236.3 5.3 %copy-start.11 = (bf16[192,1536]{1,0:T(8,128)(2,1)S(1)}, bf16[192,1536]{1,0:T(8,128)(2,1)}, u32[]{:S(2)}) copy-start(bf16[192,1536]{1,0:T(8,128)(2,1)} %get-tuple-element.26) | copy-start | bytes 1769476

commit v8 on v7

--- a/solution.py
+++ b/solution.py
@@ -296,12 +296,16 @@
         - out_normed * jnp.mean(token_delta * out_normed, axis=1, keepdims=True)
     )
     residual_delta = residual_delta.astype(jnp.bfloat16)
-    return normed, preact, activated, residual_delta
-
-
-def backward_half(normed, preact, activated, residual_delta, down_weight):
+    derivative = (
+        0.5 * (1.0 + lax.erf(preact * 0.7071067811865476))
+        + preact * jnp.exp(-0.5 * preact * preact) * 0.3989422804014327
+    )
+    return normed, derivative, activated, residual_delta
+
+
+def backward_half(normed, derivative, activated, residual_delta, down_weight):
     features = normed.shape[1]
-    hidden_units = preact.shape[1]
+    hidden_units = derivative.shape[1]
     down_scale = hidden_units ** (-0.5)
     down_gradient = (
         lax.dot_general(
@@ -314,10 +318,6 @@
             residual_delta, down_weight, (((1,), (1,)), ((), ())), preferred_element_type=jnp.float32
         )
         * down_scale
-    )
-    derivative = (
-        0.5 * (1.0 + lax.erf(preact * 0.7071067811865476))
-        + preact * jnp.exp(-0.5 * preact * preact) * 0.3989422804014327
     )
     preact_delta = (hidden_delta * derivative).astype(jnp.bfloat16)
     up_gradient = lax.dot_general(

time: 245 us -> 245 us (level)
  no operation moved by 1% of the time
where the time goes in v8:
time: 245 us
  Pallas kernels  225 us (92%)
  other arithmetic  9.86 us (4%)
  local copies, waits for them, and re-layouts  7.97 us (3%)
  between operations  2.8 us (1%)
    pallas_call x1, Pallas kernels, scatter_with_gradients(): pl.pallas_call(functools.partial(scatter_compute_kernel, n), out_shape=(j...  81.9 us
    pallas_call x1, Pallas kernels, exploit_gather(): pl.pallas_call(functools.partial(gather_kernel, members, batch_total, pat...  75.6 us
    pallas_call x1, Pallas kernels, member_call(): pl.pallas_call(functools.partial(body, n), out_shape=jax.ShapeDtypeStruct...  67 us
    broadcast_in_dim x2, other arithmetic, per_device(): return tuple((value[None] for value in up_new + down_new))  8.07 us

profile of v8, /device:TPU:1, one launch (start us, length us, event | category | flops | bytes accessed | tf_op | source)
XLA Modules:
  0.0 245.1 jit_solution(15691498208969711901)
XLA Ops:
  0.6 0.0 copy-start.4
  0.6 1.4 convert_element_type.38
  2.1 0.7 convert_element_type.39
  2.8 0.0 copy-done.4
  2.8 0.1 convert_element_type.40
  2.9 0.6 convert_element_type.41
  3.4 0.0 copy-start
  3.5 0.3 pad_maximum_fusion.send_ref
  3.8 0.3 copy-done
  4.1 67.0 %shard_map.163 = bf16[64,72,128]{2,1,0:T(8,128)(2,1)S(1)} custom-call(s32[64]{0:T(128)S(1)} %copy-done, bf16[64,72,128]{2,1,0:T(8,128)(2,1)S(1)} %pad_maximum_fusion.send_ref), custom_call_target="tpu_custom_call" | custom-call | bytes 23592960 | tf_op jit(solution)/shard_map/pallas_call | solution.py:499
  71.1 0.3 fusion.8
  71.4 0.0 copy-start.7
  71.4 1.5 reshape.24.up_ref
  72.9 1.4 reshape.25.down_ref
  74.3 0.0 copy-done.7
  74.3 0.1 copy.20
  74.4 0.0 copy-start.9
  74.4 1.2 reshape_squeeze.3.tokens_ref
  75.6 0.1 copy-done.9
  75.7 1.2 copy.21.classifier_ref
  76.9 75.6 %shard_map.164 = (bf16[64,144,128]{2,1,0:T(8,128)(2,1)}, bf16[768,1536]{1,0:T(8,128)(2,1)}, bf16[1536,768]{1,0:T(8,128)(2,1)}, bf16[784,768]{1,0:T(8,128)(2,1)},...) custom-call(s32[64]{0:T(128)} %source_ref.3, s32[4]{0:T(128)} %bitcast.40, ...), custom_call_target="tpu_custom_call" | custom-call | bytes 47185920 | tf_op jit(solution)/shard_map/pallas_call | solution.py:532
  152.5 0.0 copy-start.1
  152.5 0.0 copy-start.3
  152.5 81.9 %shard_map.165 = (f32[192,1536]{1,0:T(8,128)}, f32[384,768]{1,0:T(8,128)}, bf16[192,1536]{1,0:T(8,128)(2,1)}, bf16[384,768]{1,0:T(8,128)(2,1)}, bf16[192,1536]{1,0:T(8,128)(2,1)}, /*index=5*/bf16[384,768]{1,0:T(8,128)(2,1)}) custom-call(bf16[64,144,128]{2,1,0:T(8,128)(2,1)} %get-tuple-element.18.send_ref, bf16[784,768]{1,0:T(8,128)(2,1)} %get-tuple-element.19.normed_ref, ...), custom_call_target="tpu_custom_call" | custom-call | flops 5549064192 | bytes 47185920 | tf_op jit(solution)/shard_map/pallas_call | solution.py:463
  234.4 0.0 copy-done.1
  234.4 0.6 dynamic_slice.3
  237.0 0.0 copy-done.3
  237.0 0.0 copy-start.2
  237.0 0.0 copy-start.5
  237.0 0.0 copy-start.6
  237.0 0.0 copy-start.8
  237.0 0.0 copy-start.10
  237.0 0.0 copy-start.11
  237.0 5.3 %fusion.6 = (f32[1,384,768]{2,1,0:T(8,128)}, f32[1,384,768]{2,1,0:T(8,128)}, bf16[1,384,768]{2,1,0:T(8,128)(2,1)}) fusion(f32[384,768]{1,0:T(8,128)} %get-tuple-element.28, bf16[384,768]{1,0:T(8,128)(2,1)} %get-tuple-element.29, pred[]{:T(512)S(6)} %eq.3, f32[1,384,768]{2,1,0:T(8,128)} %param.23, f32[]{:T(128)} %bitcast.35, ...), kind=kLoop, calls=%fused_computation.15 | loop fusion | flops 5898240 | bytes 8257545 | tf_op jit(solution)/shard_map/broadcast_in_dim | solution.py:647
  242.3 0.0 copy-done.2
  242.3 0.0 copy-done.5
  242.3 0.0 copy-done.6
  242.3 0.0 copy-done.8
  242.4 0.0 copy-done.10
  242.4 0.0 copy-done.11
  242.4 2.8 %fusion.7 = (f32[1,192,1536]{2,1,0:T(8,128)}, f32[1,192,1536]{2,1,0:T(8,128)}, bf16[1,192,1536]{2,1,0:T(8,128)(2,1)}) fusion(f32[192,1536]{1,0:T(8,128)S(1)} %copy-done.8, bf16[192,1536]{1,0:T(8,128)(2,1)S(1)} %copy-done.11, pred[]{:T(512)S(6)} %eq.3, f32[1,192,1536]{2,1,0:T(8,128)S(1)} %copy-done.6, f32[]{:T(128)} %bitcast.34, ...), kind=kLoop, calls=%fused_computation.16 | loop fusion | flops 5898240 | bytes 8257545 | tf_op jit(solution)/shard_map/broadcast_in_dim | solution.py:647
Async XLA Ops:
  0.6 2.2 copy-start.4
  3.4 0.7 copy-start
  71.4 2.9 %copy-start.7 = (bf16[1,4,196,768]{3,1,2,0:T(4,128)(2,1)S(1)}, bf16[1,4,196,768]{3,1,2,0:T(4,128)(2,1)}, u32[]{:S(2)}) copy-start(bf16[1,4,196,768]{3,1,2,0:T(4,128)(2,1)} %param.12) | copy-start | bytes 3612676
  74.4 1.3 copy-start.9
  152.5 81.9 %copy-start.1 = (s32[64]{0:T(128)S(1)}, s32[64]{0:T(128)}, u32[]{:S(2)}) copy-start(s32[64]{0:T(128)} %source_ref.3) | copy-start | bytes 772
  152.5 84.5 %copy-start.3 = (bf16[384,768]{1,0:T(8,128)(2,1)S(1)}, bf16[384,768]{1,0:T(8,128)(2,1)}, u32[]{:S(2)}) copy-start(bf16[384,768]{1,0:T(8,128)(2,1)} %reshape.25.down_ref) | copy-start | bytes 1769476
  237.0 5.4 %copy-start.2 = (bf16[192,1536]{1,0:T(8,128)(2,1)S(1)}, bf16[192,1536]{1,0:T(8,128)(2,1)}, u32[]{:S(2)}) copy-start(bf16[192,1536]{1,0:T(8,128)(2,1)} %reshape.24.up_ref) | copy-start | bytes 1769476
  237.0 5.4 %copy-start.5 = (f32[1,192,1536]{2,1,0:T(8,128)S(1)}, f32[1,192,1536]{2,1,0:T(8,128)}, u32[]{:S(2)}) copy-start(f32[1,192,1536]{2,1,0:T(8,128)} %param.18) | copy-start | bytes 3538948
  237.0 5.3 %copy-start.6 = (f32[1,192,1536]{2,1,0:T(8,128)S(1)}, f32[1,192,1536]{2,1,0:T(8,128)}, u32[]{:S(2)}) copy-start(f32[1,192,1536]{2,1,0:T(8,128)} %param.20) | copy-start | bytes 3538948
  237.0 5.3 %copy-start.8 = (f32[192,1536]{1,0:T(8,128)S(1)}, f32[192,1536]{1,0:T(8,128)}, u32[]{:S(2)}) copy-start(f32[192,1536]{1,0:T(8,128)} %get-tuple-element.25) | copy-start | bytes 3538948
  237.0 5.3 %copy-start.10 = (bf16[192,1536]{1,0:T(8,128)(2,1)S(1)}, bf16[192,1536]{1,0:T(8,128)(2,1)}, u32[]{:S(2)}) copy-start(bf16[192,1536]{1,0:T(8,128)(2,1)} %get-tuple-element.24) | copy-start | bytes 1769476
  237.0 5.3 %copy-start.11 = (bf16[192,1536]{1,0:T(8,128)(2,1)S(1)}, bf16[192,1536]{1,0:T(8,128)(2,1)}, u32[]{:S(2)}) copy-start(bf16[192,1536]{1,0:T(8,128)(2,1)} %get-tuple-element.26) | copy-start | bytes 1769476

commit v9 on v7

--- a/solution.py
+++ b/solution.py
@@ -355,7 +355,9 @@
 
     chunk = send_ref.shape[1]
 
-    def copy(k):
+    def copy(j):
+        odd = j % 2
+        k = odd * (j // 2 + 1) + (1 - odd) * (n - j // 2)
         target = lax.rem(me + k, n)
         return pltpu.make_async_remote_copy(
             src_ref=send_ref.at[target],

time: 245 us -> 243 us (level)
  Pallas kernels: 224 us -> 221 us
where the time goes in v9:
time: 243 us; the launch traced here: 242 us
  Pallas kernels  221 us (91%)
  other arithmetic  9.86 us (4%)
  local copies, waits for them, and re-layouts  7.97 us (3%)
  between operations  2.8 us (1%)
    pallas_call x1, Pallas kernels, scatter_with_gradients(): pl.pallas_call(functools.partial(scatter_compute_kernel, n), out_shape=(j...  79.7 us
    pallas_call x1, Pallas kernels, exploit_gather(): pl.pallas_call(functools.partial(gather_kernel, members, batch_total, pat...  74.8 us
    pallas_call x1, Pallas kernels, member_call(): pl.pallas_call(functools.partial(body, n), out_shape=jax.ShapeDtypeStruct...  67 us
    broadcast_in_dim x2, other arithmetic, per_device(): return tuple((value[None] for value in up_new + down_new))  8.07 us

profile of v9, /device:TPU:1, one launch (start us, length us, event | category | flops | bytes accessed | tf_op | source)
XLA Modules:
  0.0 242.1 jit_solution(15762939886043133412)
XLA Ops:
  0.6 0.0 copy-start.4
  0.6 1.4 convert_element_type.38
  2.1 0.7 convert_element_type.39
  2.8 0.0 copy-done.4
  2.8 0.1 convert_element_type.40
  2.9 0.6 convert_element_type.41
  3.4 0.0 copy-start
  3.5 0.3 pad_maximum_fusion.send_ref
  3.8 0.3 copy-done
  4.1 67.0 %shard_map.163 = bf16[64,72,128]{2,1,0:T(8,128)(2,1)S(1)} custom-call(s32[64]{0:T(128)S(1)} %copy-done, bf16[64,72,128]{2,1,0:T(8,128)(2,1)S(1)} %pad_maximum_fusion.send_ref), custom_call_target="tpu_custom_call" | custom-call | bytes 23592960 | tf_op jit(solution)/shard_map/pallas_call | solution.py:501
  71.1 0.3 fusion.8
  71.4 0.0 copy-start.7
  71.4 1.5 reshape.24.up_ref
  72.9 1.4 reshape.25.down_ref
  74.3 0.0 copy-done.7
  74.3 0.1 copy.20
  74.4 0.0 copy-start.9
  74.4 1.2 reshape_squeeze.3.tokens_ref
  75.6 0.1 copy-done.9
  75.7 1.2 copy.21.classifier_ref
  76.9 74.8 %shard_map.164 = (bf16[64,144,128]{2,1,0:T(8,128)(2,1)}, bf16[768,1536]{1,0:T(8,128)(2,1)}, bf16[1536,768]{1,0:T(8,128)(2,1)}, bf16[784,768]{1,0:T(8,128)(2,1)},...) custom-call(s32[64]{0:T(128)} %source_ref.3, s32[4]{0:T(128)} %bitcast.40, ...), custom_call_target="tpu_custom_call" | custom-call | bytes 47185920 | tf_op jit(solution)/shard_map/pallas_call | solution.py:534
  151.6 0.0 copy-start.1
  151.6 0.0 copy-start.3
  151.7 79.7 %shard_map.165 = (f32[192,1536]{1,0:T(8,128)}, f32[384,768]{1,0:T(8,128)}, bf16[192,1536]{1,0:T(8,128)(2,1)}, bf16[384,768]{1,0:T(8,128)(2,1)}, bf16[192,1536]{1,0:T(8,128)(2,1)}, /*index=5*/bf16[384,768]{1,0:T(8,128)(2,1)}) custom-call(bf16[64,144,128]{2,1,0:T(8,128)(2,1)} %get-tuple-element.18.send_ref, bf16[784,768]{1,0:T(8,128)(2,1)} %get-tuple-element.19.normed_ref, ...), custom_call_target="tpu_custom_call" | custom-call | flops 5549064192 | bytes 47185920 | tf_op jit(solution)/shard_map/pallas_call | solution.py:465
  231.4 0.0 copy-done.1
  231.4 0.6 dynamic_slice.3
  233.9 0.0 copy-done.3
  233.9 0.0 copy-start.2
  234.0 0.0 copy-start.5
  234.0 0.0 copy-start.6
  234.0 0.0 copy-start.8
  234.0 0.0 copy-start.10
  234.0 0.0 copy-start.11
  234.0 5.3 %fusion.6 = (f32[1,384,768]{2,1,0:T(8,128)}, f32[1,384,768]{2,1,0:T(8,128)}, bf16[1,384,768]{2,1,0:T(8,128)(2,1)}) fusion(f32[384,768]{1,0:T(8,128)} %get-tuple-element.28, bf16[384,768]{1,0:T(8,128)(2,1)} %get-tuple-element.29, pred[]{:T(512)S(6)} %eq.3, f32[1,384,768]{2,1,0:T(8,128)} %param.23, f32[]{:T(128)} %bitcast.35, ...), kind=kLoop, calls=%fused_computation.15 | loop fusion | flops 5898240 | bytes 8257545 | tf_op jit(solution)/shard_map/broadcast_in_dim | solution.py:649
  239.3 0.0 copy-done.2
  239.3 0.0 copy-done.5
  239.3 0.0 copy-done.6
  239.3 0.0 copy-done.8
  239.3 0.0 copy-done.10
  239.3 0.0 copy-done.11
  239.3 2.8 %fusion.7 = (f32[1,192,1536]{2,1,0:T(8,128)}, f32[1,192,1536]{2,1,0:T(8,128)}, bf16[1,192,1536]{2,1,0:T(8,128)(2,1)}) fusion(f32[192,1536]{1,0:T(8,128)S(1)} %copy-done.8, bf16[192,1536]{1,0:T(8,128)(2,1)S(1)} %copy-done.11, pred[]{:T(512)S(6)} %eq.3, f32[1,192,1536]{2,1,0:T(8,128)S(1)} %copy-done.6, f32[]{:T(128)} %bitcast.34, ...), kind=kLoop, calls=%fused_computation.16 | loop fusion | flops 5898240 | bytes 8257545 | tf_op jit(solution)/shard_map/broadcast_in_dim | solution.py:649
Async XLA Ops:
  0.6 2.2 copy-start.4
  3.4 0.7 copy-start
  71.4 2.9 %copy-start.7 = (bf16[1,4,196,768]{3,1,2,0:T(4,128)(2,1)S(1)}, bf16[1,4,196,768]{3,1,2,0:T(4,128)(2,1)}, u32[]{:S(2)}) copy-start(bf16[1,4,196,768]{3,1,2,0:T(4,128)(2,1)} %param.12) | copy-start | bytes 3612676
  74.4 1.3 copy-start.9
  151.6 79.8 %copy-start.1 = (s32[64]{0:T(128)S(1)}, s32[64]{0:T(128)}, u32[]{:S(2)}) copy-start(s32[64]{0:T(128)} %source_ref.3) | copy-start | bytes 772
  151.6 82.3 %copy-start.3 = (bf16[384,768]{1,0:T(8,128)(2,1)S(1)}, bf16[384,768]{1,0:T(8,128)(2,1)}, u32[]{:S(2)}) copy-start(bf16[384,768]{1,0:T(8,128)(2,1)} %reshape.25.down_ref) | copy-start | bytes 1769476
  233.9 5.4 %copy-start.2 = (bf16[192,1536]{1,0:T(8,128)(2,1)S(1)}, bf16[192,1536]{1,0:T(8,128)(2,1)}, u32[]{:S(2)}) copy-start(bf16[192,1536]{1,0:T(8,128)(2,1)} %reshape.24.up_ref) | copy-start | bytes 1769476
  234.0 5.4 %copy-start.5 = (f32[1,192,1536]{2,1,0:T(8,128)S(1)}, f32[1,192,1536]{2,1,0:T(8,128)}, u32[]{:S(2)}) copy-start(f32[1,192,1536]{2,1,0:T(8,128)} %param.18) | copy-start | bytes 3538948
  234.0 5.3 %copy-start.6 = (f32[1,192,1536]{2,1,0:T(8,128)S(1)}, f32[1,192,1536]{2,1,0:T(8,128)}, u32[]{:S(2)}) copy-start(f32[1,192,1536]{2,1,0:T(8,128)} %param.20) | copy-start | bytes 3538948
  234.0 5.3 %copy-start.8 = (f32[192,1536]{1,0:T(8,128)S(1)}, f32[192,1536]{1,0:T(8,128)}, u32[]{:S(2)}) copy-start(f32[192,1536]{1,0:T(8,128)} %get-tuple-element.25) | copy-start | bytes 3538948
  234.0 5.3 %copy-start.10 = (bf16[192,1536]{1,0:T(8,128)(2,1)S(1)}, bf16[192,1536]{1,0:T(8,128)(2,1)}, u32[]{:S(2)}) copy-start(bf16[192,1536]{1,0:T(8,128)(2,1)} %get-tuple-element.24) | copy-start | bytes 1769476
  234.0 5.3 %copy-start.11 = (bf16[192,1536]{1,0:T(8,128)(2,1)S(1)}, bf16[192,1536]{1,0:T(8,128)(2,1)}, u32[]{:S(2)}) copy-start(bf16[192,1536]{1,0:T(8,128)(2,1)} %get-tuple-element.26) | copy-start | bytes 1769476
